TPU v7x, 128 devices: a whole 4x4x4 slice. The times are simulated.
128 devices in a mesh: val: 4 (over x_hi, core), cond: 8 (over z, x_lo), grid: 4 (over y).
Axes of the slice: x: 4 (x_hi: 2, x_lo: 2; x = x_hi * 2 + x_lo), y: 4, z: 4, core: 2. Of those that a mesh axis runs over, the one named last changes fastest.
Arguments:
- valence_orbitals: bfloat16 [16, 96, 9216], P('val', 'grid'), may hold values from -6 to 6
- conduction_orbitals: bfloat16 [32, 96, 9216], P('cond', 'grid'), may hold values from -6 to 6
- valence_energy: float32 [16], replicated, may hold values from -12 to -1
- conduction_energy: float32 [32], replicated, may hold values from 0.5 to 10
- grid_index: int32 [6144], replicated, may hold values from 0 to 884735, as said below
Outputs:
- response: float32 [2, 6144, 6144], P(None, ('val', 'grid'), 'cond')
Inputs may be any that keep to these rules, and one draw needn't show every extreme that they name: `grid_index`: distinct flat points of the 96 x 96 x 96 frequency grid.
All inputs are finite; a program needn't handle non-finite values.
Results may differ from a plain program's by a relative error of at most 0.0098.
Values may be sent and summed in bfloat16 or wider, within the bound.
No kernel may reach another device: no remote copies, remote signals or barrier semaphores. Data moves between devices by JAX's collectives and lax.ppermute only.
A program may use at most 128 MiB of HBM per device.

v0:
```python
import math

import jax
import jax.numpy as jnp
from jax import lax
from jax.sharding import PartitionSpec as P

NGRID = 96
NG = 6144


freq_squared = 4.0


def line_tables(points):
    indices = jnp.arange(points, dtype=jnp.int32)
    phases = indices[:, None] * indices[None, :] % points
    angles = phases.astype(jnp.float32) * (2.0 * math.pi / points)
    return (jnp.cos(angles).astype(jnp.bfloat16), (-jnp.sin(angles)).astype(jnp.bfloat16))


def plane_pass(products):
    line_cos, line_sin = line_tables(NGRID)
    z_table = jnp.concatenate([line_cos, line_sin], axis=1)
    row_total = products.shape[0]
    z_part = jnp.dot(
        products.reshape(row_total * NGRID, NGRID), z_table, preferred_element_type=jnp.float32
    )
    z_part = z_part.astype(jnp.bfloat16).reshape(row_total, NGRID, 2 * NGRID)
    first = jnp.einsum("ryk,yp->rpk", z_part, line_cos, preferred_element_type=jnp.float32)
    second = jnp.einsum("ryk,yp->rpk", z_part, line_sin, preferred_element_type=jnp.float32)
    plane_real = first[..., :NGRID] - second[..., NGRID:]
    plane_imag = second[..., :NGRID] + first[..., NGRID:]
    return jnp.concatenate([plane_real, plane_imag], axis=-1).astype(jnp.bfloat16)


def band_spectra(orbital, conduction_part):
    products = (orbital.astype(jnp.float32)[None] * conduction_part.astype(jnp.float32)).astype(
        jnp.bfloat16
    )
    band_total = conduction_part.shape[0]
    depth = conduction_part.shape[1]
    spectra = plane_pass(products.reshape(band_total * depth, NGRID, NGRID))
    return spectra.reshape(band_total, depth, NGRID, 2 * NGRID)


def line_pick(pieces, grid_index, row_offset):
    line_cos, line_sin = line_tables(NGRID)
    pair_total = pieces.shape[0]
    local_rows = pieces.shape[2]
    split = pieces.reshape(pair_total, NGRID, local_rows, 2, NGRID)
    table_rows = jnp.transpose(split, (2, 4, 1, 0, 3)).reshape(
        local_rows * NGRID, NGRID, pair_total * 2
    )
    plane_size = NGRID * NGRID
    vector_total = grid_index.shape[0]
    line_number = grid_index // plane_size
    remainder = grid_index % plane_size
    local_row = remainder // NGRID - row_offset
    column = remainder % NGRID
    inside = (local_row >= 0) & (local_row < local_rows)
    row_index = jnp.clip(local_row, 0, local_rows - 1) * NGRID + column
    block = math.gcd(vector_total, 512)
    count = vector_total // block
    scale = NGRID ** (-1.5)
    factor = jnp.where(inside, scale, 0.0).astype(jnp.float32)
    frequencies = jnp.arange(NGRID, dtype=jnp.int32)

    def one_block(item):
        lines, picks, keep = item
        picked = jnp.take(table_rows, picks, axis=0).reshape(block, NGRID, pair_total, 2)
        onehot = (lines[:, None] == frequencies[None, :]).astype(jnp.bfloat16)
        cos_pick = jnp.dot(onehot, line_cos.T, preferred_element_type=jnp.float32).astype(
            jnp.bfloat16
        )
        sin_pick = jnp.dot(onehot, line_sin.T, preferred_element_type=jnp.float32).astype(
            jnp.bfloat16
        )
        real_part = picked[..., 0]
        imag_part = picked[..., 1]
        real_out = jnp.einsum(
            "jx,jxp->jp", cos_pick, real_part, preferred_element_type=jnp.float32
        ) - jnp.einsum("jx,jxp->jp", sin_pick, imag_part, preferred_element_type=jnp.float32)
        imag_out = jnp.einsum(
            "jx,jxp->jp", sin_pick, real_part, preferred_element_type=jnp.float32
        ) + jnp.einsum("jx,jxp->jp", cos_pick, imag_part, preferred_element_type=jnp.float32)
        return jnp.stack([real_out * keep[:, None], imag_out * keep[:, None]])

    blocks = lax.map(
        one_block,
        (
            line_number.reshape(count, block),
            row_index.reshape(count, block),
            factor.reshape(count, block),
        ),
    )
    result = jnp.transpose(blocks, (1, 3, 0, 2)).reshape(2, pair_total, vector_total)
    return result.astype(jnp.bfloat16)


def local(valence_orbitals, conduction_orbitals, valence_energy, conduction_energy, grid_index):
    valence_groups = lax.axis_size("val")
    conduction_groups = lax.axis_size("cond")
    grid_groups = lax.axis_size("grid")
    valence_local = valence_orbitals.shape[0]
    conduction_local = conduction_orbitals.shape[0]
    pair_count = valence_local * conduction_local
    slab_depth = valence_orbitals.shape[1]

    def one_valence(orbital):
        return band_spectra(orbital, conduction_orbitals)

    spectra = lax.map(one_valence, valence_orbitals)
    spectra = spectra.reshape(pair_count, slab_depth, NGRID, 2 * NGRID)
    row_offset = lax.axis_index("grid") * (NGRID // grid_groups)
    partial_values = line_pick(
        lax.all_to_all(spectra, "grid", split_axis=2, concat_axis=1, tiled=True),
        grid_index,
        row_offset,
    )
    pair_values = lax.psum(partial_values.astype(jnp.float32).astype(jnp.bfloat16), "grid")
    delta = valence_energy[:, None] - conduction_energy[None, :]
    all_pairs = valence_energy.shape[0] * conduction_energy.shape[0]
    weights = 4.0 * delta / (delta * delta + freq_squared) / math.sqrt(all_pairs)
    weights = weights.reshape(valence_groups, valence_local, conduction_groups, conduction_local)
    weights = jnp.transpose(weights, (0, 2, 1, 3)).reshape(all_pairs)
    row_width = NG // (valence_groups * grid_groups)
    split_view = pair_values.reshape(2, pair_count, valence_groups, grid_groups, row_width)
    grid_rows = lax.dynamic_index_in_dim(split_view, lax.axis_index("grid"), 3, keepdims=False)
    everything = lax.all_gather(
        grid_rows.reshape(2, pair_count, valence_groups * row_width),
        ("val", "cond"),
        axis=1,
        tiled=True,
    )
    row_values = lax.dynamic_slice_in_dim(
        everything, lax.axis_index("val") * row_width, row_width, 2
    )
    scaled_rows = (row_values.astype(jnp.float32) * weights[None, :, None]).astype(jnp.bfloat16)
    by_column = lax.all_to_all(pair_values, "cond", split_axis=2, concat_axis=1, tiled=True)
    contract = (((0,), (0,)), ((), ()))
    piece = lax.all_gather(by_column, "val", axis=1, tiled=True)
    real_sum = lax.dot_general(
        scaled_rows[0], piece[0], contract, preferred_element_type=jnp.float32
    )
    real_sum = real_sum + lax.dot_general(
        scaled_rows[1], piece[1], contract, preferred_element_type=jnp.float32
    )
    imag_sum = lax.dot_general(
        scaled_rows[1], piece[0], contract, preferred_element_type=jnp.float32
    )
    imag_sum = imag_sum - lax.dot_general(
        scaled_rows[0], piece[1], contract, preferred_element_type=jnp.float32
    )
    return jnp.stack([real_sum, imag_sum])


def solution(mesh):
    return jax.shard_map(
        local,
        mesh=mesh,
        in_specs=(P("val", "grid", None), P("cond", "grid", None), P(), P(), P()),
        out_specs=P(None, ("val", "grid"), "cond"),
        check_vma=False,
    )
```

profile of v0, /device:TPU:1, one launch (start us, length us, event | category | flops | bytes accessed | tf_op | source)
XLA Modules:
  0.0 897.4 jit_solution(11764834540841196857)
XLA Ops:
  6.5 128.8 %while.23 = (s32[]{:T(128)}, bf16[4,4,24,96,192]{4,2,1,0,3:T(8,128)(2,1)}, bf16[4,24,9216]{2,1,0:T(8,128)(2,1)}, bf16[4,24,9216]{2,1,0:T(8,128)(2,1)}, s32[]{:T(128)}) while((s32[]{:T(128)}, bf16[4,4,24,96,192]{4,2,1,0,3:T(8,128)(2,1)}, bf16[4,24,9216]{2,1,0:T(8,128)(2,1)}, bf16[4,24,9216]{2,1,0:T(8,128)(2,1)}, s32[]{:T(128)}) %tuple.68), condition=%wide.region_1.2_spmd, body=%wide.region_0.1_spmd.sunk | while | flops 1034855424 | bytes 90169952 | solution.py:113
  135.3 7.7 all-to-all-start
  144.5 204.8 %all-to-all-done = bf16[16,24,96,192]{3,1,0,2:T(8,128)(2,1)} async-done(((bf16[16,24,96,192]{3,1,0,2:T(8,128)(2,1)}), bf16[16,24,96,192]{3,1,0,2:T(8,128)(2,1)}, u32[]{:S(2)}, u32[]{:S(2)}) %all-to-all-start) | async-done | bytes 14155808 | tf_op jit(solution)/shard_map/all_to_all | solution.py:117
  349.3 35.3 %copy.48 = bf16[16,4,24,24,192]{4,3,2,1,0:T(8,128)(2,1)} copy(bf16[16,4,24,24,192]{4,2,0,3,1:T(8,128)(2,1)} %bitcast.10) | data formatting | bytes 28311552 | tf_op jit(solution)/shard_map/all_to_all | solution.py:117
  384.6 29.6 %reshape.152 = bf16[16,96,24,2,96]{4,3,2,1,0:T(2,128)(2,1)} reshape(bf16[16,4,24,24,192]{4,3,2,1,0:T(8,128)(2,1)} %copy.48) | data formatting | bytes 28311552 | tf_op jit(solution)/shard_map/reshape | solution.py:51
  414.2 60.5 %copy.73 = bf16[24,96,96,16,2]{2,4,3,1,0:T(2,128)(2,1)} copy(bf16[24,96,96,16,2]{1,4,0,2,3:T(2,128)(2,1)} %bitcast.126) | data formatting | bytes 28311552
  474.7 250.2 %while.24 = (s32[]{:T(128)}, bf16[12,2,512,16]{2,3,1,0:T(8,128)(2,1)S(1)}, s32[12,512]{1,0:T(8,128)}, s32[12,512]{1,0:T(8,128)S(1)}, bf16[2304,96,32]{1,2,0:T(8,128)(2,1)}, /*index=5*/f32[12,512]{1,0:T(8,128)}, s32[]{:T(128)}) while((s32[]{:T(128)}, bf16[12,2,512,16]{2,3,1,0:T(8,128)(2,1)S(1)}, s32[12,512]{1,0:T(8,128)}, ...), condition=%wide.region_3.4_spmd.clone, body=%wide.region_2.3_spmd.clone.sunk | while | flops 28887552 | bytes 29686932 | solution.py:89
  475.3 9.6 %gather_fusion = bf16[512,96,32]{1,2,0:T(8,128)(2,1)} fusion(bf16[2304,96,32]{1,2,0:T(8,128)(2,1)} %get-tuple-element.309, s32[1024]{0:T(1024)S(1)} %pad_clamp_fusion.2), kind=kCustom, calls=%fused_computation.clone.clone.1 | custom fusion | bytes 6293504 | tf_op jit(solution)/shard_map/while/body/eval_jaxpr/jit(_take)/gather | solution.py:71
  496.1 9.6 %gather_fusion = bf16[512,96,32]{1,2,0:T(8,128)(2,1)} fusion(bf16[2304,96,32]{1,2,0:T(8,128)(2,1)} %get-tuple-element.309, s32[1024]{0:T(1024)S(1)} %pad_clamp_fusion.2), kind=kCustom, calls=%fused_computation.clone.clone.1 | custom fusion | bytes 6293504 | tf_op jit(solution)/shard_map/while/body/eval_jaxpr/jit(_take)/gather | solution.py:71
  517.0 9.6 %gather_fusion = bf16[512,96,32]{1,2,0:T(8,128)(2,1)} fusion(bf16[2304,96,32]{1,2,0:T(8,128)(2,1)} %get-tuple-element.309, s32[1024]{0:T(1024)S(1)} %pad_clamp_fusion.2), kind=kCustom, calls=%fused_computation.clone.clone.1 | custom fusion | bytes 6293504 | tf_op jit(solution)/shard_map/while/body/eval_jaxpr/jit(_take)/gather | solution.py:71
  537.8 9.6 %gather_fusion = bf16[512,96,32]{1,2,0:T(8,128)(2,1)} fusion(bf16[2304,96,32]{1,2,0:T(8,128)(2,1)} %get-tuple-element.309, s32[1024]{0:T(1024)S(1)} %pad_clamp_fusion.2), kind=kCustom, calls=%fused_computation.clone.clone.1 | custom fusion | bytes 6293504 | tf_op jit(solution)/shard_map/while/body/eval_jaxpr/jit(_take)/gather | solution.py:71
  558.7 9.6 %gather_fusion = bf16[512,96,32]{1,2,0:T(8,128)(2,1)} fusion(bf16[2304,96,32]{1,2,0:T(8,128)(2,1)} %get-tuple-element.309, s32[1024]{0:T(1024)S(1)} %pad_clamp_fusion.2), kind=kCustom, calls=%fused_computation.clone.clone.1 | custom fusion | bytes 6293504 | tf_op jit(solution)/shard_map/while/body/eval_jaxpr/jit(_take)/gather | solution.py:71
  579.5 9.6 %gather_fusion = bf16[512,96,32]{1,2,0:T(8,128)(2,1)} fusion(bf16[2304,96,32]{1,2,0:T(8,128)(2,1)} %get-tuple-element.309, s32[1024]{0:T(1024)S(1)} %pad_clamp_fusion.2), kind=kCustom, calls=%fused_computation.clone.clone.1 | custom fusion | bytes 6293504 | tf_op jit(solution)/shard_map/while/body/eval_jaxpr/jit(_take)/gather | solution.py:71
  600.4 9.6 %gather_fusion = bf16[512,96,32]{1,2,0:T(8,128)(2,1)} fusion(bf16[2304,96,32]{1,2,0:T(8,128)(2,1)} %get-tuple-element.309, s32[1024]{0:T(1024)S(1)} %pad_clamp_fusion.2), kind=kCustom, calls=%fused_computation.clone.clone.1 | custom fusion | bytes 6293504 | tf_op jit(solution)/shard_map/while/body/eval_jaxpr/jit(_take)/gather | solution.py:71
  621.2 9.6 %gather_fusion = bf16[512,96,32]{1,2,0:T(8,128)(2,1)} fusion(bf16[2304,96,32]{1,2,0:T(8,128)(2,1)} %get-tuple-element.309, s32[1024]{0:T(1024)S(1)} %pad_clamp_fusion.2), kind=kCustom, calls=%fused_computation.clone.clone.1 | custom fusion | bytes 6293504 | tf_op jit(solution)/shard_map/while/body/eval_jaxpr/jit(_take)/gather | solution.py:71
  642.1 9.6 %gather_fusion = bf16[512,96,32]{1,2,0:T(8,128)(2,1)} fusion(bf16[2304,96,32]{1,2,0:T(8,128)(2,1)} %get-tuple-element.309, s32[1024]{0:T(1024)S(1)} %pad_clamp_fusion.2), kind=kCustom, calls=%fused_computation.clone.clone.1 | custom fusion | bytes 6293504 | tf_op jit(solution)/shard_map/while/body/eval_jaxpr/jit(_take)/gather | solution.py:71
  662.9 9.6 %gather_fusion = bf16[512,96,32]{1,2,0:T(8,128)(2,1)} fusion(bf16[2304,96,32]{1,2,0:T(8,128)(2,1)} %get-tuple-element.309, s32[1024]{0:T(1024)S(1)} %pad_clamp_fusion.2), kind=kCustom, calls=%fused_computation.clone.clone.1 | custom fusion | bytes 6293504 | tf_op jit(solution)/shard_map/while/body/eval_jaxpr/jit(_take)/gather | solution.py:71
  683.8 9.6 %gather_fusion = bf16[512,96,32]{1,2,0:T(8,128)(2,1)} fusion(bf16[2304,96,32]{1,2,0:T(8,128)(2,1)} %get-tuple-element.309, s32[1024]{0:T(1024)S(1)} %pad_clamp_fusion.2), kind=kCustom, calls=%fused_computation.clone.clone.1 | custom fusion | bytes 6293504 | tf_op jit(solution)/shard_map/while/body/eval_jaxpr/jit(_take)/gather | solution.py:71
  704.6 9.6 %gather_fusion = bf16[512,96,32]{1,2,0:T(8,128)(2,1)} fusion(bf16[2304,96,32]{1,2,0:T(8,128)(2,1)} %get-tuple-element.309, s32[1024]{0:T(1024)S(1)} %pad_clamp_fusion.2), kind=kCustom, calls=%fused_computation.clone.clone.1 | custom fusion | bytes 6293504 | tf_op jit(solution)/shard_map/while/body/eval_jaxpr/jit(_take)/gather | solution.py:71
  725.7 41.6 %all-reduce.2.cloned.1.call-done = bf16[2,16,6144]{2,1,0:T(8,128)(2,1)} async-done(((bf16[2,16,6144]{2,1,0:T(8,128)(2,1)}), bf16[2,16,6144]{2,1,0:T(8,128)(2,1)}) %all-reduce.2.cloned.1.call-update) | async-done | bytes 393232 | tf_op jit(solution)/shard_map/psum | solution.py:121
  779.4 12.1 %all_to_all.33 = bf16[8,2,12288]{2,1,0:T(2,128)(2,1)} all-to-all(bf16[8,2,12288]{2,1,0:T(2,128)(2,1)S(1)} %reshape.183), channel_id=1, replica_groups=mesh['val'=4,'cond'=8,'grid'=4] {'cond'}, dimensions={0} | all-to-all | bytes 786432 | tf_op jit(solution)/shard_map/all_to_all | solution.py:140
  791.5 10.2 %reshape.184 = bf16[6144,2,16]{2,1,0:T(2,128)(2,1)S(1)} reshape(bf16[8,2,12288]{2,1,0:T(2,128)(2,1)} %all_to_all.33) | data formatting | bytes 786432
  806.9 51.1 %all-gather.3.cloned.1.call-done = bf16[2,512,1536]{2,1,0:T(8,128)(2,1)} async-done(((bf16[2,16,1536]{2,1,0:T(8,128)(2,1)}), bf16[2,512,1536]{2,1,0:T(8,128)(2,1)}) %all-gather.3.cloned.1.call-update) | async-done | bytes 3145744 | tf_op jit(solution)/shard_map/all_gather | solution.py:130
  859.4 25.5 %all-gather.5.cloned.1.call-done = bf16[2,512,768]{2,1,0:T(8,128)(2,1)} async-done(((bf16[2,128,768]{2,1,0:T(8,128)(2,1)}), bf16[2,512,768]{2,1,0:T(8,128)(2,1)}) %all-gather.5.cloned.1.call-update) | async-done | bytes 1572880 | tf_op jit(solution)/shard_map/all_gather | solution.py:142
  (294 shorter events, 289.2 us)
Async XLA Ops:
  19.7 4.1 copy-start
  51.8 4.1 copy-start
  84.0 4.1 copy-start
  116.2 4.1 copy-start
  135.3 7.8 copy-start.2
  135.3 213.9 %all-to-all-start = ((bf16[16,24,96,192]{3,1,0,2:T(8,128)(2,1)}), bf16[16,24,96,192]{3,1,0,2:T(8,128)(2,1)}, u32[]{:S(2)}, u32[]{:S(2)}) async-start(bf16[16,24,96,192]{3,1,0,2:T(8,128)(2,1)} %bitcast.127), calls=%async_computation | async-start | bytes 37748736 | tf_op jit(solution)/shard_map/all_to_all | solution.py:117
  143.1 624.3 %all-reduce.2.cloned.1.call-start = ((), (), s32[]{:S(2)}) async-start(), calls=%async_computation.2 | async-start | bytes 786432 | tf_op jit(solution)/shard_map/psum | solution.py:121
  491.2 4.3 copy-start.4
  512.0 4.3 copy-start.4
  532.9 4.3 copy-start.4
  553.7 4.3 copy-start.4
  574.6 4.3 copy-start.4
  595.4 4.3 copy-start.4
  616.3 4.3 copy-start.4
  637.1 4.3 copy-start.4
  658.0 4.3 copy-start.4
  678.8 4.3 copy-start.4
  699.7 4.3 copy-start.4
  720.5 4.3 copy-start.4
  725.7 132.3 %all-gather.3.cloned.1.call-start = ((), (), s32[]{:S(2)}) async-start(), calls=%async_computation.3 | async-start | bytes 3244032 | tf_op jit(solution)/shard_map/all_gather | solution.py:130
  770.0 114.9 %all-gather.5.cloned.1.call-start = ((), (), s32[]{:S(2)}) async-start(), calls=%async_computation.4 | async-start | bytes 1966080 | tf_op jit(solution)/shard_map/all_gather | solution.py:142
  791.5 15.0 %copy-start.5 = (f32[32]{0:T(128)S(1)}, f32[32]{0:T(128)}, u32[]{:S(2)}) copy-start(f32[32]{0:T(128)} %param.12) | copy-start | bytes 388
  791.5 15.1 %copy-start.6 = (f32[16]{0:T(128)S(1)}, f32[16]{0:T(128)}, u32[]{:S(2)}) copy-start(f32[16]{0:T(128)} %param.11) | copy-start | bytes 196
  884.8 3.4 copy-start.1
  (12 other events, 7.3 us)
Sparse Core Ops, SparseCore 0:
  725.8 41.5 all-reduce.1
  770.1 87.8 all-gather.2
  859.7 25.0 all-gather.4
where the time goes:
time: 904 us; the launch traced here: 897 us
  local copies, waits for them, and re-layouts  415 us (46%)
  waiting for transfers between devices  323 us (36%)
  other arithmetic  77.3 us (9%)
  matrix products  47.5 us (5%)
  between operations  13.3 us (1%)
  blocking collectives  12.1 us (1%)
    all_to_all x1, waiting for transfers between devices, local(): lax.all_to_all(spectra, 'grid', split_axis=2, concat_axis=1, tiled=True)  205 us
    gather x24, local copies, waits for them, and re-layouts, one_block(): jnp.take(table_rows, picks, axis=0).reshape(block, NGRID, pair_total, 2)  184 us
    unnamed x11, local copies, waits for them, and re-layouts  73.9 us
    all_gather x1, waiting for transfers between devices, local(): lax.all_gather(grid_rows.reshape(2, pair_count, valence_groups * row_widt...  51.1 us
    psum x1, waiting for transfers between devices, local(): lax.psum(partial_values.astype(jnp.float32).astype(jnp.bfloat16), 'grid')  41.6 us
    all_to_all x1, local copies, waits for them, and re-layouts, local(): lax.all_to_all(spectra, 'grid', split_axis=2, concat_axis=1, tiled=True)  35.3 us
    reshape x1, local copies, waits for them, and re-layouts, line_pick(): split = pieces.reshape(pair_total, NGRID, local_rows, 2, NGRID)  29.6 us
    all_gather x1, waiting for transfers between devices, local(): piece = lax.all_gather(by_column, 'val', axis=1, tiled=True)  25.5 us
  transfers between devices with their start and end apart: 4, of which 4 were waited for; matrix products, arithmetic and copies ran while one was open for 3% of the time, Pallas kernels for 0%

commit v1 on v0

v1 whole, which is shorter than its diff:
```python
import math

import jax
import jax.numpy as jnp
import numpy as np
from jax import lax
from jax.experimental import pallas as pl
from jax.experimental.pallas import tpu as pltpu
from jax.sharding import PartitionSpec as P

NGRID = 96
NG = 6144
HALF = NGRID // 2 + 1
PITCH = 52
ROWS = 2 * PITCH
LANES = 128
ENTRY = 6
BLOCK = 128
SUB = 32

freq_squared = 4.0


def line_tables():
    indices = np.arange(NGRID)
    phases = indices[:, None] * indices[None, :] % NGRID
    angles = phases.astype(np.float32) * np.float32(2.0 * math.pi / NGRID)
    cos = np.cos(angles).astype(np.float32).astype(jnp.bfloat16)
    sin = (-np.sin(angles)).astype(np.float32).astype(jnp.bfloat16)
    return cos, sin


def z_matrix(per_group):
    cos, sin = line_tables()
    out = np.zeros((per_group, ROWS, per_group, NGRID), cos.dtype)
    for y in range(per_group):
        out[y, :HALF, y] = cos[:HALF]
        out[y, PITCH : PITCH + HALF, y] = sin[:HALF]
    return out.reshape(per_group * ROWS, per_group * NGRID)


def y_matrix():
    cos, sin = line_tables()
    top = np.concatenate([cos.T, -(sin.T)], axis=1)
    bottom = np.concatenate([sin.T, cos.T], axis=1)
    return np.concatenate([top, bottom], axis=0)


def fold_matrix(tiles):
    out = np.zeros((tiles, SUB, SUB, 8), np.float32)
    for t in range(tiles):
        for j in range(SUB):
            out[t, j, j, t] = 1.0
            out[t, j, j, t + tiles] = 1.0
    return out.reshape(tiles * SUB, SUB * 8).astype(jnp.bfloat16)


def slab_matrix(pairs, depth):
    return np.kron(np.eye(pairs), np.ones((1, depth))).astype(jnp.bfloat16)


def tile_matrix(pairs, depth):
    return np.tile(np.eye(depth), (1, pairs)).astype(jnp.bfloat16)


def spectra_kernel(
    rows_ref, line_ref, val_ref, cond_ref, phase_ref, zmat_ref, ymat_ref, fold_ref, slab_ref,
    tile_ref, out_ref, z_scr, table_scr, phase_scr,
):
    bands_v, depth, points = val_ref.shape
    bands_c = cond_ref.shape[0]
    pairs = bands_v * bands_c
    width = pairs * depth
    tiles = width // LANES
    chunk = zmat_ref.shape[1]
    group_rows = zmat_ref.shape[0]

    wide = [
        jnp.dot(phase_ref[i], tile_ref[...], preferred_element_type=jnp.float32) for i in range(2)
    ]
    zeros = jnp.zeros((NGRID, LANES), jnp.float32)
    for sign in range(2):
        base = sign * NGRID * 16
        for s in range(8):
            t = s % tiles
            lanes = slice(t * LANES, (t + 1) * LANES)
            if s < tiles:
                first, second = wide[0][:, lanes], wide[1][:, lanes]
            elif s < 2 * tiles:
                first, second = -wide[1][:, lanes], wide[0][:, lanes]
            else:
                first, second = zeros, zeros
            if sign:
                second = -second
            phase_scr[pl.ds(base + s, NGRID, stride=16), :] = first
            phase_scr[pl.ds(base + 8 + s, NGRID, stride=16), :] = second
    table_scr[pl.ds(HALF * NGRID * ENTRY, 8), :] = jnp.zeros((8, LANES), jnp.float32)

    def z_step(i, carry):
        at = pl.multiple_of(i * chunk, LANES)
        cond = [cond_ref[c, :, pl.ds(at, chunk)].astype(jnp.float32) for c in range(bands_c)]
        parts = []
        for v in range(bands_v):
            orbital = val_ref[v, :, pl.ds(at, chunk)].astype(jnp.float32)
            parts += [orbital * cond[c] for c in range(bands_c)]
        products = jnp.concatenate(parts, axis=0).astype(jnp.bfloat16)
        z_part = lax.dot_general(
            zmat_ref[...], products, (((1,), (1,)), ((), ())), preferred_element_type=jnp.float32
        )
        row = pl.multiple_of(i * group_rows, 8)
        for t in range(tiles):
            z_scr[t, pl.ds(row, group_rows), :] = z_part[:, t * LANES : (t + 1) * LANES]
        return carry

    lax.fori_loop(0, points // chunk, z_step, 0)

    def y_step(q, carry):
        z_part = jnp.concatenate(
            [
                jnp.concatenate(
                    [
                        z_scr[t, pl.ds(q + part * PITCH, NGRID, stride=ROWS), :]
                        for t in range(tiles)
                    ],
                    axis=1,
                )
                for part in range(2)
            ],
            axis=0,
        ).astype(jnp.bfloat16)
        plane = jnp.dot(ymat_ref[...], z_part, preferred_element_type=jnp.float32)
        for part in range(2):
            for t in range(tiles):
                table_scr[pl.ds(q * (NGRID * ENTRY) + part * tiles + t, NGRID, stride=ENTRY), :] = (
                    plane[part * NGRID : (part + 1) * NGRID, t * LANES : (t + 1) * LANES]
                )
        return carry

    lax.fori_loop(0, HALF, y_step, 0)

    scale = NGRID ** (-1.5)

    def pick_step(i, carry):
        first = i * BLOCK
        picked = []
        for sub in range(BLOCK // SUB):
            real, imag = [], []
            for j in range(SUB):
                at = first + sub * SUB + j
                entry = table_scr[pl.ds(rows_ref[at], 8), :]
                line = pl.multiple_of(line_ref[at], 16)
                real.append(entry * phase_scr[pl.ds(line, 8), :])
                imag.append(entry * phase_scr[pl.ds(line + 8, 8), :])
            terms = jnp.concatenate(
                [jnp.concatenate(real, axis=0), jnp.concatenate(imag, axis=0)], axis=1
            ).astype(jnp.bfloat16)
            folded = jnp.dot(fold_ref[...], terms, preferred_element_type=jnp.float32)
            picked.append(
                [
                    jnp.concatenate(
                        [
                            folded[t * SUB : (t + 1) * SUB, part * LANES : (part + 1) * LANES]
                            for t in range(tiles)
                        ],
                        axis=1,
                    )
                    for part in range(2)
                ]
            )
        at = pl.multiple_of(first, BLOCK)
        for part in range(2):
            lines = jnp.concatenate([p[part] for p in picked], axis=0).astype(jnp.bfloat16)
            value = lax.dot_general(
                slab_ref[...], lines, (((1,), (1,)), ((), ())), preferred_element_type=jnp.float32
            )
            out_ref[part, :, pl.ds(at, BLOCK)] = (value * scale).astype(out_ref.dtype)
        return carry

    lax.fori_loop(0, out_ref.shape[2] // BLOCK, pick_step, 0)


def picked_partials(valence_orbitals, conduction_orbitals, grid_index, slab):
    bands_v, depth, points = valence_orbitals.shape
    bands_c = conduction_orbitals.shape[0]
    pairs = bands_v * bands_c
    tiles = pairs * depth // LANES
    cos, sin = line_tables()
    phases = lax.dynamic_slice_in_dim(
        jnp.asarray(np.stack([cos.T, sin.T])), slab * depth, depth, 2
    )
    plane_size = NGRID * NGRID
    k = grid_index // plane_size
    p = grid_index // NGRID % NGRID
    q = grid_index % NGRID
    mirrored = q >= HALF
    k = jnp.where(mirrored, (NGRID - k) % NGRID, k)
    p = jnp.where(mirrored, (NGRID - p) % NGRID, p)
    q = jnp.where(mirrored, NGRID - q, q)
    rows = (q * NGRID + p) * ENTRY
    lines = (k + jnp.where(mirrored, NGRID, 0)) * 16
    constants = [
        jnp.asarray(a)
        for a in (
            z_matrix(4), y_matrix(), fold_matrix(tiles), slab_matrix(pairs, depth),
            tile_matrix(pairs, depth),
        )
    ]
    smem = pl.BlockSpec(memory_space=pltpu.SMEM)
    vmem = pl.BlockSpec(memory_space=pltpu.VMEM)
    return pl.pallas_call(
        spectra_kernel,
        out_shape=jax.ShapeDtypeStruct((2, pairs, NG), jnp.bfloat16),
        in_specs=[smem, smem] + [vmem] * (3 + len(constants)),
        out_specs=vmem,
        scratch_shapes=[
            pltpu.VMEM((tiles, NGRID * ROWS, LANES), jnp.float32),
            pltpu.VMEM((HALF * NGRID * ENTRY + 8, LANES), jnp.float32),
            pltpu.VMEM((2 * NGRID * 16, LANES), jnp.float32),
        ],
        name="spectra",
    )(rows, lines, valence_orbitals, conduction_orbitals, phases, *constants)


def local(valence_orbitals, conduction_orbitals, valence_energy, conduction_energy, grid_index):
    valence_groups = lax.axis_size("val")
    conduction_groups = lax.axis_size("cond")
    grid_groups = lax.axis_size("grid")
    valence_local = valence_orbitals.shape[0]
    conduction_local = conduction_orbitals.shape[0]
    pair_count = valence_local * conduction_local
    partial_values = picked_partials(
        valence_orbitals, conduction_orbitals, grid_index, lax.axis_index("grid")
    )
    pair_values = lax.psum(partial_values, "grid")
    delta = valence_energy[:, None] - conduction_energy[None, :]
    all_pairs = valence_energy.shape[0] * conduction_energy.shape[0]
    weights = 4.0 * delta / (delta * delta + freq_squared) / math.sqrt(all_pairs)
    weights = weights.reshape(valence_groups, valence_local, conduction_groups, conduction_local)
    weights = jnp.transpose(weights, (0, 2, 1, 3)).reshape(all_pairs)
    row_width = NG // (valence_groups * grid_groups)
    split_view = pair_values.reshape(2, pair_count, valence_groups, grid_groups, row_width)
    grid_rows = lax.dynamic_index_in_dim(split_view, lax.axis_index("grid"), 3, keepdims=False)
    everything = lax.all_gather(
        grid_rows.reshape(2, pair_count, valence_groups * row_width),
        ("val", "cond"),
        axis=1,
        tiled=True,
    )
    row_values = lax.dynamic_slice_in_dim(
        everything, lax.axis_index("val") * row_width, row_width, 2
    )
    scaled_rows = (row_values.astype(jnp.float32) * weights[None, :, None]).astype(jnp.bfloat16)
    by_column = lax.all_to_all(pair_values, "cond", split_axis=2, concat_axis=1, tiled=True)
    contract = (((0,), (0,)), ((), ()))
    piece = lax.all_gather(by_column, "val", axis=1, tiled=True)
    real_sum = lax.dot_general(
        scaled_rows[0], piece[0], contract, preferred_element_type=jnp.float32
    )
    real_sum = real_sum + lax.dot_general(
        scaled_rows[1], piece[1], contract, preferred_element_type=jnp.float32
    )
    imag_sum = lax.dot_general(
        scaled_rows[1], piece[0], contract, preferred_element_type=jnp.float32
    )
    imag_sum = imag_sum - lax.dot_general(
        scaled_rows[0], piece[1], contract, preferred_element_type=jnp.float32
    )
    return jnp.stack([real_sum, imag_sum])


def solution(mesh):
    return jax.shard_map(
        local,
        mesh=mesh,
        in_specs=(P("val", "grid", None), P("cond", "grid", None), P(), P(), P()),
        out_specs=P(None, ("val", "grid"), "cond"),
        check_vma=False,
    )
```

time: 904 us -> 229 us (0.25)
  local copies, waits for them, and re-layouts: 415 us -> 18.8 us
  waiting for transfers between devices: 323 us -> 130 us
  other arithmetic: 77.3 us -> 4.44 us
  Pallas kernels: 0 us -> 47.1 us
  matrix products: 47.5 us -> 3.27 us
    all_to_all x1 -> x0, waiting for transfers between devices: 205 us -> none  [local(): lax.all_to_all(spectra, 'grid', split_axis=2, concat_axis=1, tiled=True)]
    gather x24 -> x0, local copies, waits for them, and re-layouts: 184 us -> none  [one_block(): jnp.take(table_rows, picks, axis=0).reshape(block, NGRID, pair_total, 2)]
    unnamed x11 -> x10, local copies, waits for them, and re-layouts: 73.9 us -> 5.61 us
    pallas_call x0 -> x1, Pallas kernels: none -> 47.1 us  [picked_partials(): pl.pallas_call(spectra_kernel, out_shape=jax.ShapeDtypeStruct((2, pairs,...]
    reshape x8 -> x0, local copies, waits for them, and re-layouts: 46.6 us -> none  [the longest x1 29.6 us: line_pick(): split = pieces.reshape(pair_total, NGRID, local_rows, 2, NGRID)]
    dot_general x36 -> x0, matrix products: 43.1 us -> none  [the longest x4 16.2 us: plane_pass(): jnp.einsum('ryk,yp->rpk', z_part, line_sin, preferred_element_type=jnp.fl...]
    all_to_all x1 -> x0, local copies, waits for them, and re-layouts: 35.3 us -> none  [local(): lax.all_to_all(spectra, 'grid', split_axis=2, concat_axis=1, tiled=True)]
    dot_general x12 -> x0, other arithmetic: 24.1 us -> none  [one_block(): jnp.einsum('jx,jxp->jp', cos_pick, real_part, preferred_element_type=jnp....]
  transfers between devices with their start and end apart: 4 -> 3, of which waited for: 4 -> 3; matrix products, arithmetic and copies ran while one was open for 3% -> 7% of each run, Pallas kernels for 0% -> 0%
where the time goes in v1:
time: 229 us
  waiting for transfers between devices  130 us (57%)
  Pallas kernels  47.1 us (21%)
  local copies, waits for them, and re-layouts  18.8 us (8%)
  between operations  13.2 us (6%)
  blocking collectives  12.2 us (5%)
  other arithmetic  4.44 us (2%)
  matrix products  3.27 us (1%)
    all_gather x1, waiting for transfers between devices, local(): lax.all_gather(grid_rows.reshape(2, pair_count, valence_groups * row_widt...  60.8 us
    pallas_call x1, Pallas kernels, picked_partials(): pl.pallas_call(spectra_kernel, out_shape=jax.ShapeDtypeStruct((2, pairs,...  47.1 us
    psum x1, waiting for transfers between devices, local(): pair_values = lax.psum(partial_values, 'grid')  43.5 us
    all_gather x1, waiting for transfers between devices, local(): piece = lax.all_gather(by_column, 'val', axis=1, tiled=True)  25.4 us
    all_to_all x1, blocking collectives, local(): lax.all_to_all(pair_values, 'cond', split_axis=2, concat_axis=1, tiled=True)  12.2 us
    unnamed x10, local copies, waits for them, and re-layouts  5.61 us
    all_to_all x1, local copies, waits for them, and re-layouts, local(): lax.all_to_all(pair_values, 'cond', split_axis=2, concat_axis=1, tiled=True)  4.79 us
  transfers between devices with their start and end apart: 3, of which 3 were waited for; matrix products, arithmetic and copies ran while one was open for 7% of the time, Pallas kernels for 0%

profile of v1, /device:TPU:1, one launch (start us, length us, event | category | flops | bytes accessed | tf_op | source)
XLA Modules:
  0.0 228.7 jit_solution(16906592563720778769)
XLA Ops:
  6.5 1.4 fusion.14
  8.0 1.5 constant_dynamic-slice_fusion.phase_ref
  9.5 47.1 %spectra.1 = bf16[2,16,6144]{2,1,0:T(8,128)(2,1)} custom-call(s32[6144]{0:T(1024)} %get-tuple-element.6.rows_ref, s32[6144]{0:T(1024)} %get-tuple-element.5.line_ref, bf16[4,24,9216]{2,1,0:T(8,128)(2,1)} %val_ref.1, bf16[4,24,9216]{2,1,0:T(8,128)(2,1)} %cond_ref.1, bf16[2,96,24]{2,1,0:T(8,128)(2,1)} %constant_dynamic-slice_fusion.phase_ref, ...), custom_call_target="tpu_custom_call" | custom-call | tf_op jit(solution)/shard_map/spectra/pallas_call | solution.py:210
  56.6 43.5 %all-reduce.2.cloned.1.call-done = bf16[2,16,6144]{2,1,0:T(8,128)(2,1)} async-done(((bf16[2,16,6144]{2,1,0:T(8,128)(2,1)}), bf16[2,16,6144]{2,1,0:T(8,128)(2,1)}) %all-reduce.2.cloned.1.call-update) | async-done | bytes 393232 | tf_op jit(solution)/shard_map/psum | solution.py:234
  100.1 1.3 reshape.30
  101.5 0.6 dynamic-slice_reduce_fusion
  102.1 0.7 reshape.31
  102.8 4.0 %copy.17 = bf16[2,16,6144]{1,0,2:T(2,128)(2,1)S(1)} copy(bf16[2,16,6144]{2,1,0:T(8,128)(2,1)S(1)} %copy-done.1) | data formatting | bytes 786432 | tf_op jit(solution)/shard_map/psum | solution.py:234
  106.8 3.3 %reshape.36 = bf16[8,2,12288]{2,1,0:T(2,128)(2,1)S(1)} reshape(bf16[6144,2,16]{2,1,0:T(2,128)(2,1)S(1)} %bitcast.27) | data formatting | bytes 786432
  110.1 12.2 %all_to_all.18 = bf16[8,2,12288]{2,1,0:T(2,128)(2,1)S(1)} all-to-all(bf16[8,2,12288]{2,1,0:T(2,128)(2,1)S(1)} %reshape.36), channel_id=1, replica_groups=mesh['val'=4,'cond'=8,'grid'=4] {'cond'}, dimensions={0} | all-to-all | bytes 786432 | tf_op jit(solution)/shard_map/all_to_all | solution.py:253
  122.3 2.3 %reshape.37 = bf16[6144,2,16]{2,1,0:T(2,128)(2,1)S(1)} reshape(bf16[8,2,12288]{2,1,0:T(2,128)(2,1)S(1)} %all_to_all.18) | data formatting | bytes 786432
  124.7 4.8 %copy.21 = bf16[2,16,8,768]{3,1,2,0:T(8,128)(2,1)} copy(bf16[2,16,8,768]{1,0,3,2:T(2,128)(2,1)S(1)} %bitcast.28) | data formatting | bytes 786432 | tf_op jit(solution)/shard_map/all_to_all | solution.py:253
  129.5 0.1 sub.48
  129.6 0.1 sub.50
  129.7 0.1 fusion.5
  129.8 0.1 reshape.33
  129.9 60.8 %all-gather.3.cloned.1.call-done = bf16[2,512,1536]{2,1,0:T(8,128)(2,1)} async-done(((bf16[2,16,1536]{2,1,0:T(8,128)(2,1)}), bf16[2,512,1536]{2,1,0:T(8,128)(2,1)}) %all-gather.3.cloned.1.call-update) | async-done | bytes 3145744 | tf_op jit(solution)/shard_map/all_gather | solution.py:243
  190.6 1.3 multiply_convert_fusion
  192.0 25.4 %all-gather.5.cloned.1.call-done = bf16[2,512,768]{2,1,0:T(8,128)(2,1)} async-done(((bf16[2,128,768]{2,1,0:T(8,128)(2,1)}), bf16[2,512,768]{2,1,0:T(8,128)(2,1)}) %all-gather.5.cloned.1.call-update) | async-done | bytes 1572880 | tf_op jit(solution)/shard_map/all_gather | solution.py:255
  217.4 1.7 fusion.2
  219.1 0.5 fusion.3
  219.6 0.5 fusion
  220.1 0.5 fusion.1
  220.7 1.6 pad_maximum_fusion
  (14 shorter events, 0.2 us)
Async XLA Ops:
  6.5 93.6 %all-reduce.2.cloned.1.call-start = ((), (), s32[]{:S(2)}) async-start(), calls=%async_computation.1 | async-start | bytes 786432 | tf_op jit(solution)/shard_map/psum | solution.py:234
  56.6 134.1 %all-gather.3.cloned.1.call-start = ((), (), s32[]{:S(2)}) async-start(), calls=%async_computation.2 | async-start | bytes 3244032 | tf_op jit(solution)/shard_map/all_gather | solution.py:243
  100.1 2.7 %copy-start.1 = (bf16[2,16,6144]{2,1,0:T(8,128)(2,1)S(1)}, bf16[2,16,6144]{2,1,0:T(8,128)(2,1)}, u32[]{:S(2)}) copy-start(bf16[2,16,6144]{2,1,0:T(8,128)(2,1)} %all-reduce.2.cloned.1.call-done) | copy-start | bytes 1179652
  102.8 114.6 %all-gather.5.cloned.1.call-start = ((), (), s32[]{:S(2)}) async-start(), calls=%async_computation.3 | async-start | bytes 1966080 | tf_op jit(solution)/shard_map/all_gather | solution.py:255
  124.6 4.8 %copy-start.2 = (f32[16]{0:T(128)S(1)}, f32[16]{0:T(128)}, u32[]{:S(2)}) copy-start(f32[16]{0:T(128)} %param.13) | copy-start | bytes 196
  124.6 4.9 %copy-start.3 = (f32[32]{0:T(128)S(1)}, f32[32]{0:T(128)}, u32[]{:S(2)}) copy-start(f32[32]{0:T(128)} %param.14) | copy-start | bytes 388
  217.4 1.8 copy-start
Sparse Core Ops, SparseCore 0:
  56.7 43.3 all-reduce.1
  102.9 87.6 all-gather.2
  192.3 24.9 all-gather.4

commit v2 on v1

--- a/solution.py
+++ b/solution.py
@@ -65,7 +65,7 @@
 
 def spectra_kernel(
     rows_ref, line_ref, val_ref, cond_ref, phase_ref, zmat_ref, ymat_ref, fold_ref, slab_ref,
-    tile_ref, out_ref, z_scr, table_scr, phase_scr,
+    tile_ref, row_out, col_out, z_scr, table_scr, phase_scr,
 ):
     bands_v, depth, points = val_ref.shape
     bands_c = cond_ref.shape[0]
@@ -167,19 +167,31 @@
                     for part in range(2)
                 ]
             )
-        at = pl.multiple_of(first, BLOCK)
+        row_block = first // row_out.shape[3]
+        row_at = pl.multiple_of(first % row_out.shape[3], BLOCK)
+        col_at = pl.multiple_of(first % col_out.shape[3], BLOCK)
+        slabs, piece = col_out.shape[1:3]
         for part in range(2):
             lines = jnp.concatenate([p[part] for p in picked], axis=0).astype(jnp.bfloat16)
             value = lax.dot_general(
                 slab_ref[...], lines, (((1,), (1,)), ((), ())), preferred_element_type=jnp.float32
             )
-            out_ref[part, :, pl.ds(at, BLOCK)] = (value * scale).astype(out_ref.dtype)
+            value = value * scale
+            row_out[
+                row_block % slabs, row_block // slabs, part * pairs : (part + 1) * pairs,
+                pl.ds(row_at, BLOCK),
+            ] = value.astype(row_out.dtype)
+            for h in range(pairs // piece):
+                col_out[
+                    first // col_out.shape[3], part * (pairs // piece) + h, :, pl.ds(col_at, BLOCK)
+                ] = value[h * piece : (h + 1) * piece].astype(col_out.dtype)
         return carry
 
-    lax.fori_loop(0, out_ref.shape[2] // BLOCK, pick_step, 0)
-
-
-def picked_partials(valence_orbitals, conduction_orbitals, grid_index, slab):
+    lax.fori_loop(0, NG // BLOCK, pick_step, 0)
+
+
+def picked_partials(valence_orbitals, conduction_orbitals, grid_index, slab, groups):
+    val_groups, cond_groups, slabs = groups
     bands_v, depth, points = valence_orbitals.shape
     bands_c = conduction_orbitals.shape[0]
     pairs = bands_v * bands_c
@@ -209,9 +221,16 @@
     vmem = pl.BlockSpec(memory_space=pltpu.VMEM)
     return pl.pallas_call(
         spectra_kernel,
-        out_shape=jax.ShapeDtypeStruct((2, pairs, NG), jnp.bfloat16),
+        out_shape=[
+            jax.ShapeDtypeStruct(
+                (slabs, val_groups, 2 * pairs, NG // (val_groups * slabs)), jnp.bfloat16
+            ),
+            jax.ShapeDtypeStruct(
+                (cond_groups, slabs, 2 * pairs // slabs, NG // cond_groups), jnp.bfloat16
+            ),
+        ],
         in_specs=[smem, smem] + [vmem] * (3 + len(constants)),
-        out_specs=vmem,
+        out_specs=[vmem, vmem],
         scratch_shapes=[
             pltpu.VMEM((tiles, NGRID * ROWS, LANES), jnp.float32),
             pltpu.VMEM((HALF * NGRID * ENTRY + 8, LANES), jnp.float32),
@@ -221,51 +240,83 @@
     )(rows, lines, valence_orbitals, conduction_orbitals, phases, *constants)
 
 
+def swap(value, axis, partner, first):
+    count = lax.axis_size(axis)
+    other = lax.ppermute(value, axis, [(i, partner(i)) for i in range(count)])
+    return jnp.where(
+        first, jnp.concatenate([value, other], 0), jnp.concatenate([other, value], 0)
+    )
+
+
+def row_values(partials):
+    v, c, g = (lax.axis_index(name) for name in ("val", "cond", "grid"))
+    slabs, groups, lines, width = partials.shape
+    total = lax.dynamic_index_in_dim(partials, g, 0, keepdims=False).astype(jnp.float32)
+    for step in range(1, slabs):
+        piece = lax.dynamic_index_in_dim(partials, (g + step) % slabs, 0, keepdims=False)
+        ring = [(i, (i + step) % slabs) for i in range(slabs)]
+        total = total + lax.ppermute(piece, "grid", ring).astype(jnp.float32)
+    total = total.astype(jnp.bfloat16)
+    pieces = [lax.dynamic_index_in_dim(total, v, 0, keepdims=False)]
+    for bits in range(1, groups):
+        piece = lax.dynamic_index_in_dim(total, v ^ bits, 0, keepdims=False)
+        pieces.append(lax.ppermute(piece, "val", [(i, i ^ bits) for i in range(groups)]))
+    value = jnp.stack(pieces).reshape(2, 2, lines, width)
+    value = jnp.where(v % 2 == 0, value, value[:, ::-1])
+    value = jnp.where(v // 2 == 0, value, value[::-1])
+    value = value.reshape(1, groups, lines, width)
+    value = swap(value, "cond", lambda i: i ^ 1, c % 2 == 0)
+    value = swap(value, "cond", lambda i: i ^ 2, c // 2 % 2 == 0)
+    return swap(value, "cond", lambda i: (3 - i // 2) * 2 + i % 2, c // 4 == 0)
+
+
+def column_values(partials):
+    v, g = lax.axis_index("val"), lax.axis_index("grid")
+    groups, slabs, piece, width = partials.shape
+    received = lax.all_to_all(
+        partials.reshape(groups * slabs, piece, width), ("cond", "grid"), 0, 0, tiled=True
+    )
+    value = jnp.sum(received.reshape(groups, slabs, piece, width).astype(jnp.float32), 1)
+    value = value.astype(jnp.bfloat16).reshape(1, groups * piece, width)
+    value = swap(value, "val", lambda i: i ^ 2, v // 2 == 0)
+    value = swap(value, "grid", lambda i: i ^ 1, g % 2 == 0)
+    value = swap(value, "grid", lambda i: 3 - i, g // 2 == 0)
+    value = swap(value, "val", lambda i: i ^ 1, v % 2 == 0)
+    return value.reshape(-1, width)
+
+
+def row_order(value):
+    return jnp.transpose(value, (2, 3, 1, 0, 4, 5))
+
+
 def local(valence_orbitals, conduction_orbitals, valence_energy, conduction_energy, grid_index):
-    valence_groups = lax.axis_size("val")
-    conduction_groups = lax.axis_size("cond")
-    grid_groups = lax.axis_size("grid")
+    groups = tuple(lax.axis_size(name) for name in ("val", "cond", "grid"))
+    val_groups, cond_groups, slabs = groups
     valence_local = valence_orbitals.shape[0]
     conduction_local = conduction_orbitals.shape[0]
-    pair_count = valence_local * conduction_local
-    partial_values = picked_partials(
-        valence_orbitals, conduction_orbitals, grid_index, lax.axis_index("grid")
-    )
-    pair_values = lax.psum(partial_values, "grid")
+    row_partials, column_partials = picked_partials(
+        valence_orbitals, conduction_orbitals, grid_index, lax.axis_index("grid"), groups
+    )
+    rows = row_values(row_partials)
+    columns = column_values(column_partials)
     delta = valence_energy[:, None] - conduction_energy[None, :]
     all_pairs = valence_energy.shape[0] * conduction_energy.shape[0]
     weights = 4.0 * delta / (delta * delta + freq_squared) / math.sqrt(all_pairs)
-    weights = weights.reshape(valence_groups, valence_local, conduction_groups, conduction_local)
-    weights = jnp.transpose(weights, (0, 2, 1, 3)).reshape(all_pairs)
-    row_width = NG // (valence_groups * grid_groups)
-    split_view = pair_values.reshape(2, pair_count, valence_groups, grid_groups, row_width)
-    grid_rows = lax.dynamic_index_in_dim(split_view, lax.axis_index("grid"), 3, keepdims=False)
-    everything = lax.all_gather(
-        grid_rows.reshape(2, pair_count, valence_groups * row_width),
-        ("val", "cond"),
-        axis=1,
-        tiled=True,
-    )
-    row_values = lax.dynamic_slice_in_dim(
-        everything, lax.axis_index("val") * row_width, row_width, 2
-    )
-    scaled_rows = (row_values.astype(jnp.float32) * weights[None, :, None]).astype(jnp.bfloat16)
-    by_column = lax.all_to_all(pair_values, "cond", split_axis=2, concat_axis=1, tiled=True)
-    contract = (((0,), (0,)), ((), ()))
-    piece = lax.all_gather(by_column, "val", axis=1, tiled=True)
-    real_sum = lax.dot_general(
-        scaled_rows[0], piece[0], contract, preferred_element_type=jnp.float32
-    )
-    real_sum = real_sum + lax.dot_general(
-        scaled_rows[1], piece[1], contract, preferred_element_type=jnp.float32
-    )
-    imag_sum = lax.dot_general(
-        scaled_rows[1], piece[0], contract, preferred_element_type=jnp.float32
-    )
-    imag_sum = imag_sum - lax.dot_general(
-        scaled_rows[0], piece[1], contract, preferred_element_type=jnp.float32
-    )
-    return jnp.stack([real_sum, imag_sum])
+    weights = weights.reshape(val_groups, valence_local, cond_groups, conduction_local)
+    weights = jnp.transpose(weights, (2, 0, 1, 3)).reshape(cond_groups, val_groups, 1, -1)
+    weights = jnp.concatenate([weights, weights], axis=2)
+    width = rows.shape[-1]
+    split = (cond_groups, 2, val_groups // 2, slabs, rows.shape[2] // slabs)
+    scaled = rows.reshape(split + (width,)).astype(jnp.float32) * weights.reshape(split + (1,))
+    scaled = row_order(scaled.astype(jnp.bfloat16))
+    swapped = jnp.concatenate([scaled[:, slabs // 2 :], -scaled[:, : slabs // 2]], axis=1)
+    left = jnp.concatenate(
+        [scaled.reshape(2 * all_pairs, width), swapped.reshape(2 * all_pairs, width)], axis=1
+    )
+    response = lax.dot_general(
+        left, columns, (((0,), (0,)), ((), ())), preferred_element_type=jnp.float32
+    )
+    return response.reshape(2, width, columns.shape[1])
 
 
 def solution(mesh):

time: 229 us -> 107 us (0.47)
  waiting for transfers between devices: 130 us -> 12.3 us
  starting transfers between devices: 0.09 us -> 33.3 us
  between operations: 13.2 us -> 0.3 us
  local copies, waits for them, and re-layouts: 18.8 us -> 6.16 us
  blocking collectives: 12.2 us -> 0 us
    all_gather x2 -> x0, waiting for transfers between devices: 86.1 us -> none  [the longest x1 60.8 us: local(): lax.all_gather(grid_rows.reshape(2, pair_count, valence_groups * row_widt...]
    psum x1 -> x0, waiting for transfers between devices: 43.5 us -> none  [local(): pair_values = lax.psum(partial_values, 'grid')]
    ppermute x0 -> x13, starting transfers between devices: none -> 25.8 us  [the longest x7 15.9 us: swap(): other = lax.ppermute(value, axis, [(i, partner(i)) for i in range(count)])]
    ppermute x0 -> x13, waiting for transfers between devices: none -> 12.3 us  [the longest x7 8.38 us: swap(): other = lax.ppermute(value, axis, [(i, partner(i)) for i in range(count)])]
    all_to_all x1 -> x0, blocking collectives: 12.2 us -> none  [local(): lax.all_to_all(pair_values, 'cond', split_axis=2, concat_axis=1, tiled=True)]
    all_to_all x0 -> x1, starting transfers between devices: none -> 7.48 us  [column_values(): lax.all_to_all(partials.reshape(groups * slabs, piece, width), ('cond', '...]
    all_to_all x1 -> x0, local copies, waits for them, and re-layouts: 4.79 us -> none  [local(): lax.all_to_all(pair_values, 'cond', split_axis=2, concat_axis=1, tiled=True)]
    unnamed x10 -> x6, local copies, waits for them, and re-layouts: 5.61 us -> 1.16 us
  transfers between devices with their start and end apart: 3 -> 14, of which waited for: 3 -> 5; matrix products, arithmetic and copies ran while one was open for 7% -> 4% of each run, Pallas kernels for 0% -> 0%
where the time goes in v2:
time: 107 us; the launch traced here: 106 us
  Pallas kernels  47.3 us (44%)
  starting transfers between devices  33.3 us (31%)
  waiting for transfers between devices  12.3 us (11%)
  local copies, waits for them, and re-layouts  6.16 us (6%)
  other arithmetic  3.74 us (3%)
  matrix products  2.79 us (3%)
    pallas_call x1, Pallas kernels, picked_partials(): pl.pallas_call(spectra_kernel, out_shape=[jax.ShapeDtypeStruct((slabs, va...  47.3 us
    ppermute x7, starting transfers between devices, swap(): other = lax.ppermute(value, axis, [(i, partner(i)) for i in range(count)])  15.9 us
    ppermute x7, waiting for transfers between devices, swap(): other = lax.ppermute(value, axis, [(i, partner(i)) for i in range(count)])  8.38 us
    all_to_all x1, starting transfers between devices, column_values(): lax.all_to_all(partials.reshape(groups * slabs, piece, width), ('cond', '...  7.48 us
    ppermute x3, starting transfers between devices, row_values(): total = total + lax.ppermute(piece, 'grid', ring).astype(jnp.float32)  5.26 us
    ppermute x3, starting transfers between devices, row_values(): lax.ppermute(piece, 'val', [(i, i ^ bits) for i in range(groups)])  4.58 us
    ppermute x3, waiting for transfers between devices, row_values(): lax.ppermute(piece, 'val', [(i, i ^ bits) for i in range(groups)])  3.86 us
    dot_general x1, matrix products, local(): lax.dot_general(left, columns, (((0,), (0,)), ((), ())), preferred_elemen...  2.79 us
  transfers between devices with their start and end apart: 14, of which 5 were waited for; matrix products, arithmetic and copies ran while one was open for 4% of the time, Pallas kernels for 0%

profile of v2, /device:TPU:1, one launch (start us, length us, event | category | flops | bytes accessed | tf_op | source)
XLA Modules:
  0.0 105.8 jit_solution(13710911035560040256)
XLA Ops:
  0.0 1.4 %fusion.11 = (s32[6144]{0:T(1024)}, s32[6144]{0:T(1024)}) fusion(s32[6144]{0:T(1024)} %param.15), kind=kLoop, calls=%fused_computation.40 | loop fusion | flops 301056 | bytes 73728 | tf_op jit(solution)/shard_map/mul | solution.py:212
  1.4 1.5 %constant_dynamic-slice_fusion.1.phase_ref = bf16[2,96,24]{2,1,0:T(8,128)(2,1)} fusion(bf16[2,96,96]{2,1,0:T(8,128)(2,1)} %constant.177.clone, s32[]{:T(128)S(6)} %select_n.227), kind=kLoop, calls=%fused_computation.62 | loop fusion | bytes 18436 | tf_op jit(solution)/shard_map/dynamic_slice | solution.py:200
  2.9 47.3 %spectra.1 = (bf16[4,4,32,384]{3,2,1,0:T(8,128)(2,1)}, bf16[8,4,8,768]{3,2,1,0:T(8,128)(2,1)}) custom-call(s32[6144]{0:T(1024)} %get-tuple-element.19.rows_ref, s32[6144]{0:T(1024)} %get-tuple-element.18.line_ref, bf16[4,24,9216]{2,1,0:T(8,128)(2,1)} %val_ref.1, bf16[4,24,9216]{2,1,0:T(8,128)(2,1)} %cond_ref.1, ...), custom_call_target="tpu_custom_call" | custom-call | tf_op jit(solution)/shard_map/spectra/pallas_call | solution.py:222
  50.2 1.0 dynamic-slice_bitcast_fusion.2
  51.2 2.2 %collective-permute-start = (bf16[4,32,384]{2,1,0:T(8,128)(2,1)S(1)}, bf16[4,32,384]{2,1,0:T(8,128)(2,1)S(1)}, u32[]{:S(2)}, u32[]{:S(2)}) collective-permute-start(bf16[4,32,384]{2,1,0:T(8,128)(2,1)S(1)} %get-tuple-element.11), channel_id=1, source_target_pairs={{0,1},{1,2},{2,3},{3,0},{4,5},{5,6},{6,7},{7,4},{8,9},{9,10},{10,1... | collective-permute-start | bytes 294920 | tf_op jit(solution)/shard_map/ppermute | solution.py:258
  53.4 1.5 %collective-permute-start.2 = (bf16[4,32,384]{2,1,0:T(8,128)(2,1)S(1)}, bf16[4,32,384]{2,1,0:T(8,128)(2,1)S(1)}, u32[]{:S(2)}, u32[]{:S(2)}) collective-permute-start(bf16[4,32,384]{2,1,0:T(8,128)(2,1)S(1)} %get-tuple-element.12), channel_id=1, source_target_pairs={{0,3},{1,0},{2,1},{3,2},{4,7},{5,4},{6,5},{7,6},{8,11},{9,8},{10,9... | collective-permute-start | bytes 294920 | tf_op jit(solution)/shard_map/ppermute | solution.py:258
  54.9 1.6 %collective-permute-start.1 = (bf16[4,32,384]{2,1,0:T(8,128)(2,1)S(1)}, bf16[4,32,384]{2,1,0:T(8,128)(2,1)S(1)}, u32[]{:S(2)}, u32[]{:S(2)}) collective-permute-start(bf16[4,32,384]{2,1,0:T(8,128)(2,1)S(1)} %get-tuple-element.13), channel_id=1, source_target_pairs={{0,2},{1,3},{2,0},{3,1},{4,6},{5,7},{6,4},{7,5},{8,10},{9,11},{10,... | collective-permute-start | bytes 294920 | tf_op jit(solution)/shard_map/ppermute | solution.py:258
  56.5 7.5 %all-to-all-start = ((bf16[32,8,768]{2,1,0:T(8,128)(2,1)}), bf16[32,8,768]{2,1,0:T(8,128)(2,1)S(1)}, u32[]{:S(2)}, u32[]{:S(2)}) async-start(bf16[32,8,768]{2,1,0:T(8,128)(2,1)} %bitcast.47), calls=%async_computation | async-start | bytes 786432 | tf_op jit(solution)/shard_map/all_to_all | solution.py:276
  64.5 1.0 fusion.3
  65.5 4.1 %collective-permute-start.5 = (bf16[32,384]{1,0:T(8,128)(2,1)S(1)}, bf16[32,384]{1,0:T(8,128)(2,1)S(1)}, u32[]{:S(2)}, u32[]{:S(2)}) collective-permute-start(bf16[32,384]{1,0:T(8,128)(2,1)S(1)} %get-tuple-element.15), channel_id=1, source_target_pairs={{0,96},{32,64},{64,32},{96,0},{1,97},{33,65},{65,33},{97,1},{2,98}... | collective-permute-start | bytes 73736 | tf_op jit(solution)/shard_map/ppermute | solution.py:263
  70.2 2.2 %collective-permute-done.5 = bf16[32,384]{1,0:T(8,128)(2,1)S(1)} collective-permute-done((bf16[32,384]{1,0:T(8,128)(2,1)S(1)}, bf16[32,384]{1,0:T(8,128)(2,1)S(1)}, u32[]{:S(2)}, u32[]{:S(2)}) %collective-permute-start.5) | collective-permute-done | bytes 24608 | tf_op jit(solution)/shard_map/ppermute | solution.py:263
  72.4 1.7 %collective-permute-done.4 = bf16[32,384]{1,0:T(8,128)(2,1)S(1)} collective-permute-done((bf16[32,384]{1,0:T(8,128)(2,1)S(1)}, bf16[32,384]{1,0:T(8,128)(2,1)S(1)}, u32[]{:S(2)}, u32[]{:S(2)}) %collective-permute-start.4) | collective-permute-done | bytes 24608 | tf_op jit(solution)/shard_map/ppermute | solution.py:263
  75.0 1.3 %collective-permute-start.6 = (bf16[1,4,32,384]{3,2,1,0:T(8,128)(2,1)S(1)}, bf16[1,4,32,384]{3,2,1,0:T(8,128)(2,1)S(1)}, u32[]{:S(2)}, u32[]{:S(2)}) collective-permute-start(bf16[1,4,32,384]{3,2,1,0:T(8,128)(2,1)S(1)} %bitcast.49), channel_id=1, source_target_pairs={{0,4},{4,0},{8,12},{12,8},{16,20},{20,16},{24,28},{28,24},{1,5},{5... | collective-permute-start | bytes 294920 | tf_op jit(solution)/shard_map/ppermute | solution.py:245
  76.4 2.8 %collective-permute-done.9 = bf16[1,64,768]{2,1,0:T(8,128)(2,1)S(1)} collective-permute-done((bf16[1,64,768]{2,1,0:T(8,128)(2,1)S(1)}, bf16[1,64,768]{2,1,0:T(8,128)(2,1)S(1)}, u32[]{:S(2)}, u32[]{:S(2)}) %collective-permute-start.9) | collective-permute-done | bytes 98336 | tf_op jit(solution)/shard_map/ppermute | solution.py:245
  79.2 2.1 %collective-permute-start.10 = (bf16[2,64,768]{2,1,0:T(8,128)(2,1)S(1)}, bf16[2,64,768]{2,1,0:T(8,128)(2,1)S(1)}, u32[]{:S(2)}, u32[]{:S(2)}) collective-permute-start(bf16[2,64,768]{2,1,0:T(8,128)(2,1)S(1)} %maximum_select_fusion.8), channel_id=1, source_target_pairs={{0,1},{1,0},{2,3},{3,2},{4,5},{5,4},{6,7},{7,6},{8,9},{9,8},{10,11... | collective-permute-start | bytes 589832 | tf_op jit(solution)/shard_map/ppermute | solution.py:245
  81.4 1.6 %collective-permute-start.7 = (bf16[2,4,32,384]{3,2,1,0:T(8,128)(2,1)S(1)}, bf16[2,4,32,384]{3,2,1,0:T(8,128)(2,1)S(1)}, u32[]{:S(2)}, u32[]{:S(2)}) collective-permute-start(bf16[2,4,32,384]{3,2,1,0:T(8,128)(2,1)S(1)} %maximum_select_fusion.7), channel_id=1, source_target_pairs={{0,8},{4,12},{8,0},{12,4},{16,24},{20,28},{24,16},{28,20},{1,9},{5... | collective-permute-start | bytes 589832 | tf_op jit(solution)/shard_map/ppermute | solution.py:245
  83.1 1.2 %collective-permute-done.10 = bf16[2,64,768]{2,1,0:T(8,128)(2,1)S(1)} collective-permute-done((bf16[2,64,768]{2,1,0:T(8,128)(2,1)S(1)}, bf16[2,64,768]{2,1,0:T(8,128)(2,1)S(1)}, u32[]{:S(2)}, u32[]{:S(2)}) %collective-permute-start.10) | collective-permute-done | bytes 196640 | tf_op jit(solution)/shard_map/ppermute | solution.py:245
  84.4 4.3 %collective-permute-start.11 = (bf16[4,64,768]{2,1,0:T(8,128)(2,1)S(1)}, bf16[4,64,768]{2,1,0:T(8,128)(2,1)S(1)}, u32[]{:S(2)}, u32[]{:S(2)}) collective-permute-start(bf16[4,64,768]{2,1,0:T(8,128)(2,1)S(1)} %maximum_select_fusion.5), channel_id=1, source_target_pairs={{0,3},{1,2},{2,1},{3,0},{4,7},{5,6},{6,5},{7,4},{8,11},{9,10},{10,... | collective-permute-start | bytes 1179656 | tf_op jit(solution)/shard_map/ppermute | solution.py:245
  88.8 2.5 %collective-permute-start.8 = (bf16[4,4,32,384]{3,2,1,0:T(8,128)(2,1)S(1)}, bf16[4,4,32,384]{3,2,1,0:T(8,128)(2,1)S(1)}, u32[]{:S(2)}, u32[]{:S(2)}) collective-permute-start(bf16[4,4,32,384]{3,2,1,0:T(8,128)(2,1)S(1)} %maximum_select_fusion.4), channel_id=1, source_target_pairs={{0,24},{4,28},{8,16},{12,20},{16,8},{20,12},{24,0},{28,4},{1,25},{... | collective-permute-start | bytes 1179656 | tf_op jit(solution)/shard_map/ppermute | solution.py:245
  91.4 4.3 %collective-permute-done.11 = bf16[4,64,768]{2,1,0:T(8,128)(2,1)S(1)} collective-permute-done((bf16[4,64,768]{2,1,0:T(8,128)(2,1)S(1)}, bf16[4,64,768]{2,1,0:T(8,128)(2,1)S(1)}, u32[]{:S(2)}, u32[]{:S(2)}) %collective-permute-start.11) | collective-permute-done | bytes 393248 | tf_op jit(solution)/shard_map/ppermute | solution.py:245
  95.8 3.2 %collective-permute-start.12 = (bf16[8,64,768]{2,1,0:T(8,128)(2,1)S(1)}, bf16[8,64,768]{2,1,0:T(8,128)(2,1)S(1)}, u32[]{:S(2)}, u32[]{:S(2)}) collective-permute-start(bf16[8,64,768]{2,1,0:T(8,128)(2,1)S(1)} %maximum_select_fusion.2), channel_id=1, source_target_pairs={{0,32},{32,0},{64,96},{96,64},{1,33},{33,1},{65,97},{97,65},{2,34}... | collective-permute-start | bytes 2359304 | tf_op jit(solution)/shard_map/ppermute | solution.py:245
  99.9 1.6 %copy.29 = bf16[768,1024]{1,0:T(8,128)(2,1)} copy(bf16[768,1024]{0,1:T(8,128)(2,1)S(1)} %maximum_bitcast_fusion) | data formatting | bytes 3145728 | tf_op jit(solution)/shard_map/dot_general | solution.py:316
  101.8 1.2 %copy-done = bf16[768,1024]{1,0:T(8,128)(2,1)S(1)} copy-done((bf16[768,1024]{1,0:T(8,128)(2,1)S(1)}, bf16[768,1024]{1,0:T(8,128)(2,1)}, u32[]{:S(2)}) %copy-start) | copy-done | bytes 1572888
  103.0 2.8 %fusion.23 = f32[2,384,768]{2,1,0:T(8,128)} fusion(bf16[2,384,1024]{2,1,0:T(8,128)(2,1)S(1)} %bitcast.44, bf16[1024,768,1]{1,0,2:T(8,128)(2,1)S(1)} %bitcast.45), kind=kOutput, calls=%fused_computation.64 | convolution fusion | flops 1207959552 | bytes 5505024 | tf_op jit(solution)/shard_map/dot_general | solution.py:316
  (48 shorter events, 3.6 us)
Async XLA Ops:
  2.9 61.0 %copy-start.1 = (f32[16]{0:T(128)S(1)}, f32[16]{0:T(128)}, u32[]{:S(2)}) copy-start(f32[16]{0:T(128)} %param.13) | copy-start | bytes 196
  2.9 61.1 %copy-start.2 = (f32[32]{0:T(128)S(1)}, f32[32]{0:T(128)}, u32[]{:S(2)}) copy-start(f32[32]{0:T(128)} %param.14) | copy-start | bytes 388
  51.2 13.3 %collective-permute-start = (bf16[4,32,384]{2,1,0:T(8,128)(2,1)S(1)}, bf16[4,32,384]{2,1,0:T(8,128)(2,1)S(1)}, u32[]{:S(2)}, u32[]{:S(2)}) collective-permute-start(bf16[4,32,384]{2,1,0:T(8,128)(2,1)S(1)} %get-tuple-element.11), channel_id=1, source_target_pairs={{0,1},{1,2},{2,3},{3,0},{4,5},{5,6},{6,7},{7,4},{8,9},{9,10},{10,1... | collective-permute-start | bytes 294920 | tf_op jit(solution)/shard_map/ppermute | solution.py:258
  53.4 11.1 %collective-permute-start.2 = (bf16[4,32,384]{2,1,0:T(8,128)(2,1)S(1)}, bf16[4,32,384]{2,1,0:T(8,128)(2,1)S(1)}, u32[]{:S(2)}, u32[]{:S(2)}) collective-permute-start(bf16[4,32,384]{2,1,0:T(8,128)(2,1)S(1)} %get-tuple-element.12), channel_id=1, source_target_pairs={{0,3},{1,0},{2,1},{3,2},{4,7},{5,4},{6,5},{7,6},{8,11},{9,8},{10,9... | collective-permute-start | bytes 294920 | tf_op jit(solution)/shard_map/ppermute | solution.py:258
  54.9 9.6 %collective-permute-start.1 = (bf16[4,32,384]{2,1,0:T(8,128)(2,1)S(1)}, bf16[4,32,384]{2,1,0:T(8,128)(2,1)S(1)}, u32[]{:S(2)}, u32[]{:S(2)}) collective-permute-start(bf16[4,32,384]{2,1,0:T(8,128)(2,1)S(1)} %get-tuple-element.13), channel_id=1, source_target_pairs={{0,2},{1,3},{2,0},{3,1},{4,6},{5,7},{6,4},{7,5},{8,10},{9,11},{10,... | collective-permute-start | bytes 294920 | tf_op jit(solution)/shard_map/ppermute | solution.py:258
  56.5 17.6 %all-to-all-start = ((bf16[32,8,768]{2,1,0:T(8,128)(2,1)}), bf16[32,8,768]{2,1,0:T(8,128)(2,1)S(1)}, u32[]{:S(2)}, u32[]{:S(2)}) async-start(bf16[32,8,768]{2,1,0:T(8,128)(2,1)} %bitcast.47), calls=%async_computation | async-start | bytes 786432 | tf_op jit(solution)/shard_map/all_to_all | solution.py:276
  65.5 6.9 %collective-permute-start.5 = (bf16[32,384]{1,0:T(8,128)(2,1)S(1)}, bf16[32,384]{1,0:T(8,128)(2,1)S(1)}, u32[]{:S(2)}, u32[]{:S(2)}) collective-permute-start(bf16[32,384]{1,0:T(8,128)(2,1)S(1)} %get-tuple-element.15), channel_id=1, source_target_pairs={{0,96},{32,64},{64,32},{96,0},{1,97},{33,65},{65,33},{97,1},{2,98}... | collective-permute-start | bytes 73736 | tf_op jit(solution)/shard_map/ppermute | solution.py:263
  69.6 4.5 %collective-permute-start.4 = (bf16[32,384]{1,0:T(8,128)(2,1)S(1)}, bf16[32,384]{1,0:T(8,128)(2,1)S(1)}, u32[]{:S(2)}, u32[]{:S(2)}) collective-permute-start(bf16[32,384]{1,0:T(8,128)(2,1)S(1)} %get-tuple-element.16), channel_id=1, source_target_pairs={{0,64},{32,96},{64,0},{96,32},{1,65},{33,97},{65,1},{97,33},{2,66}... | collective-permute-start | bytes 73736 | tf_op jit(solution)/shard_map/ppermute | solution.py:263
  70.1 4.0 %collective-permute-start.3 = (bf16[32,384]{1,0:T(8,128)(2,1)S(1)}, bf16[32,384]{1,0:T(8,128)(2,1)S(1)}, u32[]{:S(2)}, u32[]{:S(2)}) collective-permute-start(bf16[32,384]{1,0:T(8,128)(2,1)S(1)} %get-tuple-element.17), channel_id=1, source_target_pairs={{0,32},{32,0},{64,96},{96,64},{1,33},{33,1},{65,97},{97,65},{2,34}... | collective-permute-start | bytes 73736 | tf_op jit(solution)/shard_map/ppermute | solution.py:263
  74.2 5.1 %collective-permute-start.9 = (bf16[1,64,768]{2,1,0:T(8,128)(2,1)S(1)}, bf16[1,64,768]{2,1,0:T(8,128)(2,1)S(1)}, u32[]{:S(2)}, u32[]{:S(2)}) collective-permute-start(bf16[1,64,768]{2,1,0:T(8,128)(2,1)S(1)} %bitcast.53), channel_id=1, source_target_pairs={{0,64},{32,96},{64,0},{96,32},{1,65},{33,97},{65,1},{97,33},{2,66}... | collective-permute-start | bytes 294920 | tf_op jit(solution)/shard_map/ppermute | solution.py:245
  75.0 6.3 %collective-permute-start.6 = (bf16[1,4,32,384]{3,2,1,0:T(8,128)(2,1)S(1)}, bf16[1,4,32,384]{3,2,1,0:T(8,128)(2,1)S(1)}, u32[]{:S(2)}, u32[]{:S(2)}) collective-permute-start(bf16[1,4,32,384]{3,2,1,0:T(8,128)(2,1)S(1)} %bitcast.49), channel_id=1, source_target_pairs={{0,4},{4,0},{8,12},{12,8},{16,20},{20,16},{24,28},{28,24},{1,5},{5... | collective-permute-start | bytes 294920 | tf_op jit(solution)/shard_map/ppermute | solution.py:245
  79.2 5.2 %collective-permute-start.10 = (bf16[2,64,768]{2,1,0:T(8,128)(2,1)S(1)}, bf16[2,64,768]{2,1,0:T(8,128)(2,1)S(1)}, u32[]{:S(2)}, u32[]{:S(2)}) collective-permute-start(bf16[2,64,768]{2,1,0:T(8,128)(2,1)S(1)} %maximum_select_fusion.8), channel_id=1, source_target_pairs={{0,1},{1,0},{2,3},{3,2},{4,5},{5,4},{6,7},{7,6},{8,9},{9,8},{10,11... | collective-permute-start | bytes 589832 | tf_op jit(solution)/shard_map/ppermute | solution.py:245
  81.4 7.4 %collective-permute-start.7 = (bf16[2,4,32,384]{3,2,1,0:T(8,128)(2,1)S(1)}, bf16[2,4,32,384]{3,2,1,0:T(8,128)(2,1)S(1)}, u32[]{:S(2)}, u32[]{:S(2)}) collective-permute-start(bf16[2,4,32,384]{3,2,1,0:T(8,128)(2,1)S(1)} %maximum_select_fusion.7), channel_id=1, source_target_pairs={{0,8},{4,12},{8,0},{12,4},{16,24},{20,28},{24,16},{28,20},{1,9},{5... | collective-permute-start | bytes 589832 | tf_op jit(solution)/shard_map/ppermute | solution.py:245
  84.4 11.3 %collective-permute-start.11 = (bf16[4,64,768]{2,1,0:T(8,128)(2,1)S(1)}, bf16[4,64,768]{2,1,0:T(8,128)(2,1)S(1)}, u32[]{:S(2)}, u32[]{:S(2)}) collective-permute-start(bf16[4,64,768]{2,1,0:T(8,128)(2,1)S(1)} %maximum_select_fusion.5), channel_id=1, source_target_pairs={{0,3},{1,2},{2,1},{3,0},{4,7},{5,6},{6,5},{7,4},{8,11},{9,10},{10,... | collective-permute-start | bytes 1179656 | tf_op jit(solution)/shard_map/ppermute | solution.py:245
  88.8 10.3 %collective-permute-start.8 = (bf16[4,4,32,384]{3,2,1,0:T(8,128)(2,1)S(1)}, bf16[4,4,32,384]{3,2,1,0:T(8,128)(2,1)S(1)}, u32[]{:S(2)}, u32[]{:S(2)}) collective-permute-start(bf16[4,4,32,384]{3,2,1,0:T(8,128)(2,1)S(1)} %maximum_select_fusion.4), channel_id=1, source_target_pairs={{0,24},{4,28},{8,16},{12,20},{16,8},{20,12},{24,0},{28,4},{1,25},{... | collective-permute-start | bytes 1179656 | tf_op jit(solution)/shard_map/ppermute | solution.py:245
  95.8 5.7 %collective-permute-start.12 = (bf16[8,64,768]{2,1,0:T(8,128)(2,1)S(1)}, bf16[8,64,768]{2,1,0:T(8,128)(2,1)S(1)}, u32[]{:S(2)}, u32[]{:S(2)}) collective-permute-start(bf16[8,64,768]{2,1,0:T(8,128)(2,1)S(1)} %maximum_select_fusion.2), channel_id=1, source_target_pairs={{0,32},{32,0},{64,96},{96,64},{1,33},{33,1},{65,97},{97,65},{2,34}... | collective-permute-start | bytes 2359304 | tf_op jit(solution)/shard_map/ppermute | solution.py:245
  101.6 1.4 %copy-start = (bf16[768,1024]{1,0:T(8,128)(2,1)S(1)}, bf16[768,1024]{1,0:T(8,128)(2,1)}, u32[]{:S(2)}) copy-start(bf16[768,1024]{1,0:T(8,128)(2,1)} %copy.29) | copy-start | bytes 4718596

commit v3 on v2

--- a/solution.py
+++ b/solution.py
@@ -16,6 +16,10 @@
 LANES = 128
 ENTRY = 6
 BLOCK = 128
+GROUP = 4
+FREQS = HALF + 1
+YPAIRS = 5
+FETCH = 4
 SUB = 32
 
 freq_squared = 4.0
@@ -30,13 +34,13 @@
     return cos, sin
 
 
-def z_matrix(per_group):
+def z_matrix():
     cos, sin = line_tables()
-    out = np.zeros((per_group, ROWS, per_group, NGRID), cos.dtype)
-    for y in range(per_group):
+    out = np.zeros((GROUP, ROWS, GROUP, NGRID), cos.dtype)
+    for y in range(GROUP):
         out[y, :HALF, y] = cos[:HALF]
         out[y, PITCH : PITCH + HALF, y] = sin[:HALF]
-    return out.reshape(per_group * ROWS, per_group * NGRID)
+    return out.reshape(GROUP * ROWS, GROUP * NGRID)
 
 
 def y_matrix():
@@ -64,16 +68,25 @@
 
 
 def spectra_kernel(
-    rows_ref, line_ref, val_ref, cond_ref, phase_ref, zmat_ref, ymat_ref, fold_ref, slab_ref,
-    tile_ref, row_out, col_out, z_scr, table_scr, phase_scr,
+    index_ref, val_ref, cond_ref, phase_ref, zmat_ref, ymat_ref, fold_ref, slab_ref,
+    tile_ref, row_out, col_out, z_scr, table_scr, phase_scr, prod_a, prod_b, lines_a, lines_b,
+    index_a, index_b, index_sem,
 ):
+    index_scr = (index_a, index_b)
     bands_v, depth, points = val_ref.shape
     bands_c = cond_ref.shape[0]
     pairs = bands_v * bands_c
     width = pairs * depth
     tiles = width // LANES
-    chunk = zmat_ref.shape[1]
-    group_rows = zmat_ref.shape[0]
+    chunk = GROUP * NGRID
+
+    def fetch(block, slot):
+        pltpu.make_async_copy(
+            index_ref.at[pl.ds(block * FETCH, FETCH)], index_scr[slot], index_sem.at[slot]
+        ).start()
+
+    fetch(0, 0)
+    fetch(1, 1)
 
     wide = [
         jnp.dot(phase_ref[i], tile_ref[...], preferred_element_type=jnp.float32) for i in range(2)
@@ -94,89 +107,106 @@
                 second = -second
             phase_scr[pl.ds(base + s, NGRID, stride=16), :] = first
             phase_scr[pl.ds(base + 8 + s, NGRID, stride=16), :] = second
-    table_scr[pl.ds(HALF * NGRID * ENTRY, 8), :] = jnp.zeros((8, LANES), jnp.float32)
+    table_scr[pl.ds(FREQS * NGRID * ENTRY, 8), :] = jnp.zeros((8, LANES), jnp.float32)
+
+    def multiply(i, prod):
+        for half in range(2):
+            at = pl.multiple_of((2 * i + half) * chunk, LANES)
+            cond = [cond_ref[c, :, pl.ds(at, chunk)].astype(jnp.float32) for c in range(bands_c)]
+            for v in range(bands_v):
+                orbital = val_ref[v, :, pl.ds(at, chunk)].astype(jnp.float32)
+                rows = jnp.concatenate([orbital * cond[c] for c in range(bands_c)], axis=0)
+                first = half * width + v * bands_c * depth
+                prod[first : first + bands_c * depth, :] = rows.astype(jnp.bfloat16)
+
+    def z_transform(i, prod):
+        for y0, y1, k0, k1 in ((0, 2, 0, 256), (2, 3, 0, 384), (3, 4, 256, 384)):
+            z_part = lax.dot_general(
+                zmat_ref[y0 * ROWS : y1 * ROWS, k0:k1], prod[:, k0:k1],
+                (((1,), (1,)), ((), ())), preferred_element_type=jnp.float32,
+            )
+            for half in range(2):
+                row = pl.multiple_of(((2 * i + half) * GROUP + y0) * ROWS, 8)
+                for t in range(tiles):
+                    lane = half * width + t * LANES
+                    z_scr[t, pl.ds(row, (y1 - y0) * ROWS), :] = z_part[:, lane : lane + LANES]
+
+    z_last = points // (2 * chunk) - 1
+    multiply(0, prod_a)
 
     def z_step(i, carry):
-        at = pl.multiple_of(i * chunk, LANES)
-        cond = [cond_ref[c, :, pl.ds(at, chunk)].astype(jnp.float32) for c in range(bands_c)]
-        parts = []
-        for v in range(bands_v):
-            orbital = val_ref[v, :, pl.ds(at, chunk)].astype(jnp.float32)
-            parts += [orbital * cond[c] for c in range(bands_c)]
-        products = jnp.concatenate(parts, axis=0).astype(jnp.bfloat16)
-        z_part = lax.dot_general(
-            zmat_ref[...], products, (((1,), (1,)), ((), ())), preferred_element_type=jnp.float32
-        )
-        row = pl.multiple_of(i * group_rows, 8)
-        for t in range(tiles):
-            z_scr[t, pl.ds(row, group_rows), :] = z_part[:, t * LANES : (t + 1) * LANES]
+        z_transform(2 * i, prod_a)
+        multiply(2 * i + 1, prod_b)
+        z_transform(2 * i + 1, prod_b)
+        multiply(jnp.minimum(2 * i + 2, z_last), prod_a)
         return carry
 
-    lax.fori_loop(0, points // chunk, z_step, 0)
-
-    def y_step(q, carry):
-        z_part = jnp.concatenate(
-            [
-                jnp.concatenate(
-                    [
-                        z_scr[t, pl.ds(q + part * PITCH, NGRID, stride=ROWS), :]
-                        for t in range(tiles)
-                    ],
-                    axis=1,
-                )
-                for part in range(2)
-            ],
-            axis=0,
-        ).astype(jnp.bfloat16)
-        plane = jnp.dot(ymat_ref[...], z_part, preferred_element_type=jnp.float32)
-        for part in range(2):
-            for t in range(tiles):
-                table_scr[pl.ds(q * (NGRID * ENTRY) + part * tiles + t, NGRID, stride=ENTRY), :] = (
-                    plane[part * NGRID : (part + 1) * NGRID, t * LANES : (t + 1) * LANES]
-                )
+    lax.fori_loop(0, (z_last + 1) // 2, z_step, 0)
+
+    def y_step(i, carry):
+        for pair in range(YPAIRS):
+            first = (i * YPAIRS + pair) * 2
+            z_part = jnp.concatenate(
+                [
+                    jnp.concatenate(
+                        [
+                            z_scr[t, pl.ds(first + q + part * PITCH, NGRID, stride=ROWS), :]
+                            for q in range(2)
+                            for t in range(tiles)
+                        ],
+                        axis=1,
+                    )
+                    for part in range(2)
+                ],
+                axis=0,
+            ).astype(jnp.bfloat16)
+            plane = jnp.dot(ymat_ref[...], z_part, preferred_element_type=jnp.float32)
+            for q in range(2):
+                for part in range(2):
+                    for t in range(tiles):
+                        at = (first + q) * (NGRID * ENTRY) + part * tiles + t
+                        lane = (q * tiles + t) * LANES
+                        table_scr[pl.ds(at, NGRID, stride=ENTRY), :] = plane[
+                            part * NGRID : (part + 1) * NGRID, lane : lane + LANES
+                        ]
         return carry
 
-    lax.fori_loop(0, HALF, y_step, 0)
+    lax.fori_loop(0, FREQS // (2 * YPAIRS), y_step, 0)
 
     scale = NGRID ** (-1.5)
 
-    def pick_step(i, carry):
-        first = i * BLOCK
-        picked = []
+    def gather(slot, row, lines):
         for sub in range(BLOCK // SUB):
             real, imag = [], []
-            for j in range(SUB):
-                at = first + sub * SUB + j
-                entry = table_scr[pl.ds(rows_ref[at], 8), :]
-                line = pl.multiple_of(line_ref[at], 16)
+            for j in range(sub * SUB, (sub + 1) * SUB):
+                entry = table_scr[pl.ds(index_scr[slot][row, 0, j], 8), :]
+                line = pl.multiple_of(index_scr[slot][row, 1, j], 16)
                 real.append(entry * phase_scr[pl.ds(line, 8), :])
                 imag.append(entry * phase_scr[pl.ds(line + 8, 8), :])
             terms = jnp.concatenate(
                 [jnp.concatenate(real, axis=0), jnp.concatenate(imag, axis=0)], axis=1
             ).astype(jnp.bfloat16)
             folded = jnp.dot(fold_ref[...], terms, preferred_element_type=jnp.float32)
-            picked.append(
-                [
-                    jnp.concatenate(
-                        [
-                            folded[t * SUB : (t + 1) * SUB, part * LANES : (part + 1) * LANES]
-                            for t in range(tiles)
-                        ],
-                        axis=1,
-                    )
-                    for part in range(2)
-                ]
-            )
+            folded = folded.astype(jnp.bfloat16)
+            for part in range(2):
+                for t in range(tiles):
+                    first = part * BLOCK + sub * SUB
+                    lines[first : first + SUB, t * LANES : (t + 1) * LANES] = folded[
+                        t * SUB : (t + 1) * SUB, part * LANES : (part + 1) * LANES
+                    ]
+
+    def add_x(block, lines):
+        first = block * BLOCK
         row_block = first // row_out.shape[3]
         row_at = pl.multiple_of(first % row_out.shape[3], BLOCK)
         col_at = pl.multiple_of(first % col_out.shape[3], BLOCK)
         slabs, piece = col_out.shape[1:3]
+        both = lax.dot_general(
+            slab_ref[...], lines[...], (((1,), (1,)), ((), ())), preferred_element_type=jnp.float32
+        )
+        both = both * scale
         for part in range(2):
-            lines = jnp.concatenate([p[part] for p in picked], axis=0).astype(jnp.bfloat16)
-            value = lax.dot_general(
-                slab_ref[...], lines, (((1,), (1,)), ((), ())), preferred_element_type=jnp.float32
-            )
-            value = value * scale
+            value = both[:, part * BLOCK : (part + 1) * BLOCK]
             row_out[
                 row_block % slabs, row_block // slabs, part * pairs : (part + 1) * pairs,
                 pl.ds(row_at, BLOCK),
@@ -185,9 +215,29 @@
                 col_out[
                     first // col_out.shape[3], part * (pairs // piece) + h, :, pl.ds(col_at, BLOCK)
                 ] = value[h * piece : (h + 1) * piece].astype(col_out.dtype)
+
+    def await_fetch(slot):
+        pltpu.make_async_copy(
+            index_ref.at[pl.ds(0, FETCH)], index_scr[slot], index_sem.at[slot]
+        ).wait()
+
+    last = NG // (BLOCK * FETCH) - 1
+    await_fetch(0)
+    gather(0, 0, lines_a)
+    buffers = (lines_a, lines_b)
+
+    def pick_step(i, carry):
+        for n in range(2 * FETCH):
+            slot, row = (n + 1) // FETCH % 2, (n + 1) % FETCH
+            if row == 0:
+                fetch(jnp.minimum(2 * i + n // FETCH + 2, last), 1 - slot)
+                await_fetch(slot)
+            gather(slot, row, buffers[(n + 1) % 2])
+            add_x(2 * FETCH * i + n, buffers[n % 2])
         return carry
 
-    lax.fori_loop(0, NG // BLOCK, pick_step, 0)
+    lax.fori_loop(0, (last + 1) // 2, pick_step, 0)
+    await_fetch(1)
 
 
 def picked_partials(valence_orbitals, conduction_orbitals, grid_index, slab, groups):
@@ -213,11 +263,11 @@
     constants = [
         jnp.asarray(a)
         for a in (
-            z_matrix(4), y_matrix(), fold_matrix(tiles), slab_matrix(pairs, depth),
+            z_matrix(), y_matrix(), fold_matrix(tiles), slab_matrix(pairs, depth),
             tile_matrix(pairs, depth),
         )
     ]
-    smem = pl.BlockSpec(memory_space=pltpu.SMEM)
+    index = jnp.stack([rows.reshape(-1, BLOCK), lines.reshape(-1, BLOCK)], axis=1)
     vmem = pl.BlockSpec(memory_space=pltpu.VMEM)
     return pl.pallas_call(
         spectra_kernel,
@@ -229,15 +279,22 @@
                 (cond_groups, slabs, 2 * pairs // slabs, NG // cond_groups), jnp.bfloat16
             ),
         ],
-        in_specs=[smem, smem] + [vmem] * (3 + len(constants)),
+        in_specs=[pl.BlockSpec(memory_space=pl.ANY)] + [vmem] * (3 + len(constants)),
         out_specs=[vmem, vmem],
         scratch_shapes=[
             pltpu.VMEM((tiles, NGRID * ROWS, LANES), jnp.float32),
-            pltpu.VMEM((HALF * NGRID * ENTRY + 8, LANES), jnp.float32),
+            pltpu.VMEM((FREQS * NGRID * ENTRY + 8, LANES), jnp.float32),
             pltpu.VMEM((2 * NGRID * 16, LANES), jnp.float32),
+            pltpu.VMEM((2 * pairs * depth, GROUP * NGRID), jnp.bfloat16),
+            pltpu.VMEM((2 * pairs * depth, GROUP * NGRID), jnp.bfloat16),
+            pltpu.VMEM((2 * BLOCK, pairs * depth), jnp.bfloat16),
+            pltpu.VMEM((2 * BLOCK, pairs * depth), jnp.bfloat16),
+            pltpu.SMEM((FETCH, 2, BLOCK), jnp.int32),
+            pltpu.SMEM((FETCH, 2, BLOCK), jnp.int32),
+            pltpu.SemaphoreType.DMA((2,)),
         ],
         name="spectra",
-    )(rows, lines, valence_orbitals, conduction_orbitals, phases, *constants)
+    )(index, valence_orbitals, conduction_orbitals, phases, *constants)
 
 
 def swap(value, axis, partner, first):

time: 107 us -> 86.4 us (0.81)
  Pallas kernels: 47.3 us -> 26.3 us
    pallas_call x1, Pallas kernels: 47.3 us -> 26.3 us  [picked_partials(): pl.pallas_call(spectra_kernel, out_shape=[jax.ShapeDtypeStruct((slabs, va...]
  transfers between devices with their start and end apart: 14 -> 14, of which waited for: 5 -> 5; matrix products, arithmetic and copies ran while one was open for 4% -> 5% of each run, Pallas kernels for 0% -> 0%
where the time goes in v3:
time: 86.4 us; the launch traced here: 85 us
  starting transfers between devices  33.5 us (39%)
  Pallas kernels  26.3 us (30%)
  waiting for transfers between devices  12.2 us (14%)
  local copies, waits for them, and re-layouts  6.18 us (7%)
  other arithmetic  3.78 us (4%)
  matrix products  2.79 us (3%)
    pallas_call x1, Pallas kernels, picked_partials(): pl.pallas_call(spectra_kernel, out_shape=[jax.ShapeDtypeStruct((slabs, va...  26.3 us
    ppermute x7, starting transfers between devices, swap(): other = lax.ppermute(value, axis, [(i, partner(i)) for i in range(count)])  16.1 us
    ppermute x7, waiting for transfers between devices, swap(): other = lax.ppermute(value, axis, [(i, partner(i)) for i in range(count)])  8.31 us
    all_to_all x1, starting transfers between devices, column_values(): lax.all_to_all(partials.reshape(groups * slabs, piece, width), ('cond', '...  7.47 us
    ppermute x3, starting transfers between devices, row_values(): total = total + lax.ppermute(piece, 'grid', ring).astype(jnp.float32)  5.25 us
    ppermute x3, starting transfers between devices, row_values(): lax.ppermute(piece, 'val', [(i, i ^ bits) for i in range(groups)])  4.6 us
    ppermute x3, waiting for transfers between devices, row_values(): lax.ppermute(piece, 'val', [(i, i ^ bits) for i in range(groups)])  3.84 us
    dot_general x1, matrix products, local(): lax.dot_general(left, columns, (((0,), (0,)), ((), ())), preferred_elemen...  2.79 us
  transfers between devices with their start and end apart: 14, of which 5 were waited for; matrix products, arithmetic and copies ran while one was open for 5% of the time, Pallas kernels for 0%

profile of v3, /device:TPU:1, one launch (start us, length us, event | category | flops | bytes accessed | tf_op | source)
XLA Modules:
  0.0 85.0 jit_solution(13625284901370030355)
XLA Ops:
  0.8 1.5 %constant_dynamic-slice_fusion.1.phase_ref = bf16[2,96,24]{2,1,0:T(8,128)(2,1)} fusion(bf16[2,96,96]{2,1,0:T(8,128)(2,1)} %constant.177.clone, s32[]{:T(128)S(6)} %select_n.227), kind=kLoop, calls=%fused_computation.63 | loop fusion | bytes 18436 | tf_op jit(solution)/shard_map/dynamic_slice | solution.py:250
  3.0 26.3 %spectra.1 = (bf16[4,4,32,384]{3,2,1,0:T(8,128)(2,1)}, bf16[8,4,8,768]{3,2,1,0:T(8,128)(2,1)}) custom-call(s32[48,2,128]{2,1,0:T(2,128)} %pad_add_fusion.index_ref, bf16[4,24,9216]{2,1,0:T(8,128)(2,1)} %val_ref.1, bf16[4,24,9216]{2,1,0:T(8,128)(2,1)} %cond_ref.1, bf16[2,96,24]{2,1,0:T(8,128)(2,1)} %constant_dynamic-slice_fusion.1.phase_ref, ...), custom_call_target="tpu_custom_call" | custom-call | tf_op jit(solution)/shard_map/spectra/pallas_call | solution.py:272
  29.3 1.0 %dynamic-slice_bitcast_fusion.2 = (bf16[4,32,384]{2,1,0:T(8,128)(2,1)S(1)}, bf16[4,32,384]{2,1,0:T(8,128)(2,1)S(1)}, bf16[4,32,384]{2,1,0:T(8,128)(2,1)S(1)}) fusion(bf16[4,4,32,384]{3,2,1,0:T(8,128)(2,1)} %get-tuple-element.7, s32[]{:T(128)S(6)} %select_n.230, s32[]{:T(128)S(6)} %select_n.234, s32[]{:T(128)S(6)} %select_n.232), kind=kLoop, calls=%fused_computation.24 | loop fusion | bytes 589836 | tf_op jit(solution)/shard_map/jit(dynamic_index_in_dim)/squeeze | solution.py:313
  30.4 2.2 %collective-permute-start = (bf16[4,32,384]{2,1,0:T(8,128)(2,1)S(1)}, bf16[4,32,384]{2,1,0:T(8,128)(2,1)S(1)}, u32[]{:S(2)}, u32[]{:S(2)}) collective-permute-start(bf16[4,32,384]{2,1,0:T(8,128)(2,1)S(1)} %get-tuple-element.11), channel_id=1, source_target_pairs={{0,1},{1,2},{2,3},{3,0},{4,5},{5,6},{6,7},{7,4},{8,9},{9,10},{10,1... | collective-permute-start | bytes 294920 | tf_op jit(solution)/shard_map/ppermute | solution.py:315
  32.6 1.5 %collective-permute-start.2 = (bf16[4,32,384]{2,1,0:T(8,128)(2,1)S(1)}, bf16[4,32,384]{2,1,0:T(8,128)(2,1)S(1)}, u32[]{:S(2)}, u32[]{:S(2)}) collective-permute-start(bf16[4,32,384]{2,1,0:T(8,128)(2,1)S(1)} %get-tuple-element.12), channel_id=1, source_target_pairs={{0,3},{1,0},{2,1},{3,2},{4,7},{5,4},{6,5},{7,6},{8,11},{9,8},{10,9... | collective-permute-start | bytes 294920 | tf_op jit(solution)/shard_map/ppermute | solution.py:315
  34.1 1.6 %collective-permute-start.1 = (bf16[4,32,384]{2,1,0:T(8,128)(2,1)S(1)}, bf16[4,32,384]{2,1,0:T(8,128)(2,1)S(1)}, u32[]{:S(2)}, u32[]{:S(2)}) collective-permute-start(bf16[4,32,384]{2,1,0:T(8,128)(2,1)S(1)} %get-tuple-element.13), channel_id=1, source_target_pairs={{0,2},{1,3},{2,0},{3,1},{4,6},{5,7},{6,4},{7,5},{8,10},{9,11},{10,... | collective-permute-start | bytes 294920 | tf_op jit(solution)/shard_map/ppermute | solution.py:315
  35.6 7.5 %all-to-all-start = ((bf16[32,8,768]{2,1,0:T(8,128)(2,1)}), bf16[32,8,768]{2,1,0:T(8,128)(2,1)S(1)}, u32[]{:S(2)}, u32[]{:S(2)}) async-start(bf16[32,8,768]{2,1,0:T(8,128)(2,1)} %bitcast.49), calls=%async_computation | async-start | bytes 786432 | tf_op jit(solution)/shard_map/all_to_all | solution.py:333
  43.6 1.0 %fusion.3 = bf16[4,32,384]{2,1,0:T(8,128)(2,1)S(1)} fusion(bf16[4,32,384]{2,1,0:T(8,128)(2,1)S(1)} %collective-permute-done.2, bf16[4,32,384]{2,1,0:T(8,128)(2,1)S(1)} %collective-permute-done.1, bf16[4,32,384]{2,1,0:T(8,128)(2,1)S(1)} %collective-permute-done, bf16[4,4,32,384]{3,2,1,0:T(8,128)(2,1)} %get-tuple-element.7, s32[]{:T(128)S(6)} %select_n.228), kind=kLoop, calls=%fused_computation.18 | loop fusion | flops 393216 | bytes 491524 | tf_op jit(solution)/shard_map/convert_element_type | solution.py:316
  44.6 4.1 %collective-permute-start.5 = (bf16[32,384]{1,0:T(8,128)(2,1)S(1)}, bf16[32,384]{1,0:T(8,128)(2,1)S(1)}, u32[]{:S(2)}, u32[]{:S(2)}) collective-permute-start(bf16[32,384]{1,0:T(8,128)(2,1)S(1)} %get-tuple-element.15), channel_id=1, source_target_pairs={{0,96},{32,64},{64,32},{96,0},{1,97},{33,65},{65,33},{97,1},{2,98}... | collective-permute-start | bytes 73736 | tf_op jit(solution)/shard_map/ppermute | solution.py:320
  49.3 2.2 %collective-permute-done.5 = bf16[32,384]{1,0:T(8,128)(2,1)S(1)} collective-permute-done((bf16[32,384]{1,0:T(8,128)(2,1)S(1)}, bf16[32,384]{1,0:T(8,128)(2,1)S(1)}, u32[]{:S(2)}, u32[]{:S(2)}) %collective-permute-start.5) | collective-permute-done | bytes 24608 | tf_op jit(solution)/shard_map/ppermute | solution.py:320
  51.5 1.7 %collective-permute-done.4 = bf16[32,384]{1,0:T(8,128)(2,1)S(1)} collective-permute-done((bf16[32,384]{1,0:T(8,128)(2,1)S(1)}, bf16[32,384]{1,0:T(8,128)(2,1)S(1)}, u32[]{:S(2)}, u32[]{:S(2)}) %collective-permute-start.4) | collective-permute-done | bytes 24608 | tf_op jit(solution)/shard_map/ppermute | solution.py:320
  53.3 1.0 %collective-permute-start.9 = (bf16[1,64,768]{2,1,0:T(8,128)(2,1)S(1)}, bf16[1,64,768]{2,1,0:T(8,128)(2,1)S(1)}, u32[]{:S(2)}, u32[]{:S(2)}) collective-permute-start(bf16[1,64,768]{2,1,0:T(8,128)(2,1)S(1)} %bitcast.55), channel_id=1, source_target_pairs={{0,64},{32,96},{64,0},{96,32},{1,65},{33,97},{65,1},{97,33},{2,66}... | collective-permute-start | bytes 294920 | tf_op jit(solution)/shard_map/ppermute | solution.py:302
  54.3 1.2 %collective-permute-start.6 = (bf16[1,4,32,384]{3,2,1,0:T(8,128)(2,1)S(1)}, bf16[1,4,32,384]{3,2,1,0:T(8,128)(2,1)S(1)}, u32[]{:S(2)}, u32[]{:S(2)}) collective-permute-start(bf16[1,4,32,384]{3,2,1,0:T(8,128)(2,1)S(1)} %bitcast.51), channel_id=1, source_target_pairs={{0,4},{4,0},{8,12},{12,8},{16,20},{20,16},{24,28},{28,24},{1,5},{5... | collective-permute-start | bytes 294920 | tf_op jit(solution)/shard_map/ppermute | solution.py:302
  55.5 2.8 %collective-permute-done.9 = bf16[1,64,768]{2,1,0:T(8,128)(2,1)S(1)} collective-permute-done((bf16[1,64,768]{2,1,0:T(8,128)(2,1)S(1)}, bf16[1,64,768]{2,1,0:T(8,128)(2,1)S(1)}, u32[]{:S(2)}, u32[]{:S(2)}) %collective-permute-start.9) | collective-permute-done | bytes 98336 | tf_op jit(solution)/shard_map/ppermute | solution.py:302
  58.4 2.1 %collective-permute-start.10 = (bf16[2,64,768]{2,1,0:T(8,128)(2,1)S(1)}, bf16[2,64,768]{2,1,0:T(8,128)(2,1)S(1)}, u32[]{:S(2)}, u32[]{:S(2)}) collective-permute-start(bf16[2,64,768]{2,1,0:T(8,128)(2,1)S(1)} %maximum_select_fusion.8), channel_id=1, source_target_pairs={{0,1},{1,0},{2,3},{3,2},{4,5},{5,4},{6,7},{7,6},{8,9},{9,8},{10,11... | collective-permute-start | bytes 589832 | tf_op jit(solution)/shard_map/ppermute | solution.py:302
  60.5 1.6 %collective-permute-start.7 = (bf16[2,4,32,384]{3,2,1,0:T(8,128)(2,1)S(1)}, bf16[2,4,32,384]{3,2,1,0:T(8,128)(2,1)S(1)}, u32[]{:S(2)}, u32[]{:S(2)}) collective-permute-start(bf16[2,4,32,384]{3,2,1,0:T(8,128)(2,1)S(1)} %maximum_select_fusion.7), channel_id=1, source_target_pairs={{0,8},{4,12},{8,0},{12,4},{16,24},{20,28},{24,16},{28,20},{1,9},{5... | collective-permute-start | bytes 589832 | tf_op jit(solution)/shard_map/ppermute | solution.py:302
  62.3 1.3 %collective-permute-done.10 = bf16[2,64,768]{2,1,0:T(8,128)(2,1)S(1)} collective-permute-done((bf16[2,64,768]{2,1,0:T(8,128)(2,1)S(1)}, bf16[2,64,768]{2,1,0:T(8,128)(2,1)S(1)}, u32[]{:S(2)}, u32[]{:S(2)}) %collective-permute-start.10) | collective-permute-done | bytes 196640 | tf_op jit(solution)/shard_map/ppermute | solution.py:302
  63.6 4.2 %collective-permute-start.11 = (bf16[4,64,768]{2,1,0:T(8,128)(2,1)S(1)}, bf16[4,64,768]{2,1,0:T(8,128)(2,1)S(1)}, u32[]{:S(2)}, u32[]{:S(2)}) collective-permute-start(bf16[4,64,768]{2,1,0:T(8,128)(2,1)S(1)} %maximum_select_fusion.5), channel_id=1, source_target_pairs={{0,3},{1,2},{2,1},{3,0},{4,7},{5,6},{6,5},{7,4},{8,11},{9,10},{10,... | collective-permute-start | bytes 1179656 | tf_op jit(solution)/shard_map/ppermute | solution.py:302
  67.9 2.5 %collective-permute-start.8 = (bf16[4,4,32,384]{3,2,1,0:T(8,128)(2,1)S(1)}, bf16[4,4,32,384]{3,2,1,0:T(8,128)(2,1)S(1)}, u32[]{:S(2)}, u32[]{:S(2)}) collective-permute-start(bf16[4,4,32,384]{3,2,1,0:T(8,128)(2,1)S(1)} %maximum_select_fusion.4), channel_id=1, source_target_pairs={{0,24},{4,28},{8,16},{12,20},{16,8},{20,12},{24,0},{28,4},{1,25},{... | collective-permute-start | bytes 1179656 | tf_op jit(solution)/shard_map/ppermute | solution.py:302
  70.5 4.2 %collective-permute-done.11 = bf16[4,64,768]{2,1,0:T(8,128)(2,1)S(1)} collective-permute-done((bf16[4,64,768]{2,1,0:T(8,128)(2,1)S(1)}, bf16[4,64,768]{2,1,0:T(8,128)(2,1)S(1)}, u32[]{:S(2)}, u32[]{:S(2)}) %collective-permute-start.11) | collective-permute-done | bytes 393248 | tf_op jit(solution)/shard_map/ppermute | solution.py:302
  74.8 3.5 %collective-permute-start.12 = (bf16[8,64,768]{2,1,0:T(8,128)(2,1)S(1)}, bf16[8,64,768]{2,1,0:T(8,128)(2,1)S(1)}, u32[]{:S(2)}, u32[]{:S(2)}) collective-permute-start(bf16[8,64,768]{2,1,0:T(8,128)(2,1)S(1)} %maximum_select_fusion.2), channel_id=1, source_target_pairs={{0,32},{32,0},{64,96},{96,64},{1,33},{33,1},{65,97},{97,65},{2,34}... | collective-permute-start | bytes 2359304 | tf_op jit(solution)/shard_map/ppermute | solution.py:302
  79.2 1.6 %copy.29 = bf16[768,1024]{1,0:T(8,128)(2,1)} copy(bf16[768,1024]{0,1:T(8,128)(2,1)S(1)} %maximum_bitcast_fusion) | data formatting | bytes 3145728 | tf_op jit(solution)/shard_map/dot_general | solution.py:373
  81.1 1.2 %copy-done = bf16[768,1024]{1,0:T(8,128)(2,1)S(1)} copy-done((bf16[768,1024]{1,0:T(8,128)(2,1)S(1)}, bf16[768,1024]{1,0:T(8,128)(2,1)}, u32[]{:S(2)}) %copy-start) | copy-done | bytes 1572888
  82.2 2.8 %fusion.23 = f32[2,384,768]{2,1,0:T(8,128)} fusion(bf16[2,384,1024]{2,1,0:T(8,128)(2,1)S(1)} %bitcast.46, bf16[1024,768,1]{1,0,2:T(8,128)(2,1)S(1)} %bitcast.47), kind=kOutput, calls=%fused_computation.65 | convolution fusion | flops 1207959552 | bytes 5505024 | tf_op jit(solution)/shard_map/dot_general | solution.py:373
  (49 shorter events, 4.3 us)
Async XLA Ops:
  3.0 40.1 %copy-start.1 = (f32[16]{0:T(128)S(1)}, f32[16]{0:T(128)}, u32[]{:S(2)}) copy-start(f32[16]{0:T(128)} %param.13) | copy-start | bytes 196
  3.0 40.2 %copy-start.2 = (f32[32]{0:T(128)S(1)}, f32[32]{0:T(128)}, u32[]{:S(2)}) copy-start(f32[32]{0:T(128)} %param.14) | copy-start | bytes 388
  30.4 13.2 %collective-permute-start = (bf16[4,32,384]{2,1,0:T(8,128)(2,1)S(1)}, bf16[4,32,384]{2,1,0:T(8,128)(2,1)S(1)}, u32[]{:S(2)}, u32[]{:S(2)}) collective-permute-start(bf16[4,32,384]{2,1,0:T(8,128)(2,1)S(1)} %get-tuple-element.11), channel_id=1, source_target_pairs={{0,1},{1,2},{2,3},{3,0},{4,5},{5,6},{6,7},{7,4},{8,9},{9,10},{10,1... | collective-permute-start | bytes 294920 | tf_op jit(solution)/shard_map/ppermute | solution.py:315
  32.6 11.1 %collective-permute-start.2 = (bf16[4,32,384]{2,1,0:T(8,128)(2,1)S(1)}, bf16[4,32,384]{2,1,0:T(8,128)(2,1)S(1)}, u32[]{:S(2)}, u32[]{:S(2)}) collective-permute-start(bf16[4,32,384]{2,1,0:T(8,128)(2,1)S(1)} %get-tuple-element.12), channel_id=1, source_target_pairs={{0,3},{1,0},{2,1},{3,2},{4,7},{5,4},{6,5},{7,6},{8,11},{9,8},{10,9... | collective-permute-start | bytes 294920 | tf_op jit(solution)/shard_map/ppermute | solution.py:315
  34.1 9.6 %collective-permute-start.1 = (bf16[4,32,384]{2,1,0:T(8,128)(2,1)S(1)}, bf16[4,32,384]{2,1,0:T(8,128)(2,1)S(1)}, u32[]{:S(2)}, u32[]{:S(2)}) collective-permute-start(bf16[4,32,384]{2,1,0:T(8,128)(2,1)S(1)} %get-tuple-element.13), channel_id=1, source_target_pairs={{0,2},{1,3},{2,0},{3,1},{4,6},{5,7},{6,4},{7,5},{8,10},{9,11},{10,... | collective-permute-start | bytes 294920 | tf_op jit(solution)/shard_map/ppermute | solution.py:315
  35.6 17.6 %all-to-all-start = ((bf16[32,8,768]{2,1,0:T(8,128)(2,1)}), bf16[32,8,768]{2,1,0:T(8,128)(2,1)S(1)}, u32[]{:S(2)}, u32[]{:S(2)}) async-start(bf16[32,8,768]{2,1,0:T(8,128)(2,1)} %bitcast.49), calls=%async_computation | async-start | bytes 786432 | tf_op jit(solution)/shard_map/all_to_all | solution.py:333
  44.6 6.9 %collective-permute-start.5 = (bf16[32,384]{1,0:T(8,128)(2,1)S(1)}, bf16[32,384]{1,0:T(8,128)(2,1)S(1)}, u32[]{:S(2)}, u32[]{:S(2)}) collective-permute-start(bf16[32,384]{1,0:T(8,128)(2,1)S(1)} %get-tuple-element.15), channel_id=1, source_target_pairs={{0,96},{32,64},{64,32},{96,0},{1,97},{33,65},{65,33},{97,1},{2,98}... | collective-permute-start | bytes 73736 | tf_op jit(solution)/shard_map/ppermute | solution.py:320
  48.7 4.5 %collective-permute-start.4 = (bf16[32,384]{1,0:T(8,128)(2,1)S(1)}, bf16[32,384]{1,0:T(8,128)(2,1)S(1)}, u32[]{:S(2)}, u32[]{:S(2)}) collective-permute-start(bf16[32,384]{1,0:T(8,128)(2,1)S(1)} %get-tuple-element.16), channel_id=1, source_target_pairs={{0,64},{32,96},{64,0},{96,32},{1,65},{33,97},{65,1},{97,33},{2,66}... | collective-permute-start | bytes 73736 | tf_op jit(solution)/shard_map/ppermute | solution.py:320
  49.2 4.0 %collective-permute-start.3 = (bf16[32,384]{1,0:T(8,128)(2,1)S(1)}, bf16[32,384]{1,0:T(8,128)(2,1)S(1)}, u32[]{:S(2)}, u32[]{:S(2)}) collective-permute-start(bf16[32,384]{1,0:T(8,128)(2,1)S(1)} %get-tuple-element.17), channel_id=1, source_target_pairs={{0,32},{32,0},{64,96},{96,64},{1,33},{33,1},{65,97},{97,65},{2,34}... | collective-permute-start | bytes 73736 | tf_op jit(solution)/shard_map/ppermute | solution.py:320
  53.3 5.1 %collective-permute-start.9 = (bf16[1,64,768]{2,1,0:T(8,128)(2,1)S(1)}, bf16[1,64,768]{2,1,0:T(8,128)(2,1)S(1)}, u32[]{:S(2)}, u32[]{:S(2)}) collective-permute-start(bf16[1,64,768]{2,1,0:T(8,128)(2,1)S(1)} %bitcast.55), channel_id=1, source_target_pairs={{0,64},{32,96},{64,0},{96,32},{1,65},{33,97},{65,1},{97,33},{2,66}... | collective-permute-start | bytes 294920 | tf_op jit(solution)/shard_map/ppermute | solution.py:302
  54.3 6.2 %collective-permute-start.6 = (bf16[1,4,32,384]{3,2,1,0:T(8,128)(2,1)S(1)}, bf16[1,4,32,384]{3,2,1,0:T(8,128)(2,1)S(1)}, u32[]{:S(2)}, u32[]{:S(2)}) collective-permute-start(bf16[1,4,32,384]{3,2,1,0:T(8,128)(2,1)S(1)} %bitcast.51), channel_id=1, source_target_pairs={{0,4},{4,0},{8,12},{12,8},{16,20},{20,16},{24,28},{28,24},{1,5},{5... | collective-permute-start | bytes 294920 | tf_op jit(solution)/shard_map/ppermute | solution.py:302
  58.4 5.2 %collective-permute-start.10 = (bf16[2,64,768]{2,1,0:T(8,128)(2,1)S(1)}, bf16[2,64,768]{2,1,0:T(8,128)(2,1)S(1)}, u32[]{:S(2)}, u32[]{:S(2)}) collective-permute-start(bf16[2,64,768]{2,1,0:T(8,128)(2,1)S(1)} %maximum_select_fusion.8), channel_id=1, source_target_pairs={{0,1},{1,0},{2,3},{3,2},{4,5},{5,4},{6,7},{7,6},{8,9},{9,8},{10,11... | collective-permute-start | bytes 589832 | tf_op jit(solution)/shard_map/ppermute | solution.py:302
  60.5 7.3 %collective-permute-start.7 = (bf16[2,4,32,384]{3,2,1,0:T(8,128)(2,1)S(1)}, bf16[2,4,32,384]{3,2,1,0:T(8,128)(2,1)S(1)}, u32[]{:S(2)}, u32[]{:S(2)}) collective-permute-start(bf16[2,4,32,384]{3,2,1,0:T(8,128)(2,1)S(1)} %maximum_select_fusion.7), channel_id=1, source_target_pairs={{0,8},{4,12},{8,0},{12,4},{16,24},{20,28},{24,16},{28,20},{1,9},{5... | collective-permute-start | bytes 589832 | tf_op jit(solution)/shard_map/ppermute | solution.py:302
  63.6 11.1 %collective-permute-start.11 = (bf16[4,64,768]{2,1,0:T(8,128)(2,1)S(1)}, bf16[4,64,768]{2,1,0:T(8,128)(2,1)S(1)}, u32[]{:S(2)}, u32[]{:S(2)}) collective-permute-start(bf16[4,64,768]{2,1,0:T(8,128)(2,1)S(1)} %maximum_select_fusion.5), channel_id=1, source_target_pairs={{0,3},{1,2},{2,1},{3,0},{4,7},{5,6},{6,5},{7,4},{8,11},{9,10},{10,... | collective-permute-start | bytes 1179656 | tf_op jit(solution)/shard_map/ppermute | solution.py:302
  67.9 10.5 %collective-permute-start.8 = (bf16[4,4,32,384]{3,2,1,0:T(8,128)(2,1)S(1)}, bf16[4,4,32,384]{3,2,1,0:T(8,128)(2,1)S(1)}, u32[]{:S(2)}, u32[]{:S(2)}) collective-permute-start(bf16[4,4,32,384]{3,2,1,0:T(8,128)(2,1)S(1)} %maximum_select_fusion.4), channel_id=1, source_target_pairs={{0,24},{4,28},{8,16},{12,20},{16,8},{20,12},{24,0},{28,4},{1,25},{... | collective-permute-start | bytes 1179656 | tf_op jit(solution)/shard_map/ppermute | solution.py:302
  74.8 6.0 %collective-permute-start.12 = (bf16[8,64,768]{2,1,0:T(8,128)(2,1)S(1)}, bf16[8,64,768]{2,1,0:T(8,128)(2,1)S(1)}, u32[]{:S(2)}, u32[]{:S(2)}) collective-permute-start(bf16[8,64,768]{2,1,0:T(8,128)(2,1)S(1)} %maximum_select_fusion.2), channel_id=1, source_target_pairs={{0,32},{32,0},{64,96},{96,64},{1,33},{33,1},{65,97},{97,65},{2,34}... | collective-permute-start | bytes 2359304 | tf_op jit(solution)/shard_map/ppermute | solution.py:302
  80.8 1.4 %copy-start = (bf16[768,1024]{1,0:T(8,128)(2,1)S(1)}, bf16[768,1024]{1,0:T(8,128)(2,1)}, u32[]{:S(2)}) copy-start(bf16[768,1024]{1,0:T(8,128)(2,1)} %copy.29) | copy-start | bytes 4718596

commit v4 on v3

--- a/solution.py
+++ b/solution.py
@@ -7,6 +7,7 @@
 from jax.experimental import pallas as pl
 from jax.experimental.pallas import tpu as pltpu
 from jax.sharding import PartitionSpec as P
+
 
 NGRID = 96
 NG = 6144
@@ -242,7 +243,7 @@
 
 def picked_partials(valence_orbitals, conduction_orbitals, grid_index, slab, groups):
     val_groups, cond_groups, slabs = groups
-    bands_v, depth, points = valence_orbitals.shape
+    bands_v, depth, _ = valence_orbitals.shape
     bands_c = conduction_orbitals.shape[0]
     pairs = bands_v * bands_c
     tiles = pairs * depth // LANES
@@ -312,7 +313,8 @@
     for step in range(1, slabs):
         piece = lax.dynamic_index_in_dim(partials, (g + step) % slabs, 0, keepdims=False)
         ring = [(i, (i + step) % slabs) for i in range(slabs)]
-        total = total + lax.ppermute(piece, "grid", ring).astype(jnp.float32)
+        other = lax.ppermute(piece, "grid", ring)
+        total = total + other.astype(jnp.float32)
     total = total.astype(jnp.bfloat16)
     pieces = [lax.dynamic_index_in_dim(total, v, 0, keepdims=False)]
     for bits in range(1, groups):
@@ -323,8 +325,31 @@
     value = jnp.where(v // 2 == 0, value, value[::-1])
     value = value.reshape(1, groups, lines, width)
     value = swap(value, "cond", lambda i: i ^ 1, c % 2 == 0)
-    value = swap(value, "cond", lambda i: i ^ 2, c // 2 % 2 == 0)
-    return swap(value, "cond", lambda i: (3 - i // 2) * 2 + i % 2, c // 4 == 0)
+    low, high, core = c // 2 % 2, c // 4, v % 2
+    near, far = (lambda i: i ^ 2), (lambda i: (3 - i // 2) * 2 + i % 2)
+    count = lax.axis_size("cond")
+
+    def by_core(first, second):
+        return [
+            (i * count + j, i * count + (first if i % 2 == 0 else second)(j))
+            for i in range(groups)
+            for j in range(count)
+        ]
+
+    other = lax.ppermute(value, ("val", "cond"), by_core(near, far))
+    first = jnp.where(core == 0, low, high) == 0
+    own = jnp.where(first, jnp.stack([value, other]), jnp.stack([other, value]))
+    other = lax.ppermute(own, ("val", "cond"), by_core(far, near))
+    parts = []
+    for h in range(2):
+        for l in range(2):
+            mine = jnp.where(core == 0, high == h, (low == l) == (high == h))
+            if h == l:
+                parts.append(jnp.where(mine, own[h], other[h]))
+            else:
+                by_low, by_high = jnp.where(mine, own[l], other[l]), jnp.where(mine, own[h], other[h])
+                parts.append(jnp.where(core == 0, by_low, by_high))
+    return jnp.stack(parts).reshape(count, groups, lines, width)
 
 
 def column_values(partials):

time: 86.4 us -> 93.5 us (1.082); the launches traced: 85 us -> 93.1 us
  waiting for transfers between devices: 12.2 us -> 20.8 us
    ppermute x7 -> x5, waiting for transfers between devices: 8.31 us -> 16.4 us  [swap(): other = lax.ppermute(value, axis, [(i, partner(i)) for i in range(count)])]
    ppermute x3 -> x5, waiting for transfers between devices: 0.01 us -> 4.35 us  [the longest x3 3.71 us: row_values(): other = lax.ppermute(piece, 'grid', ring)]
    ppermute x7 -> x5, starting transfers between devices: 16.1 us -> 12.2 us  [swap(): other = lax.ppermute(value, axis, [(i, partner(i)) for i in range(count)])]
    ppermute x3, waiting for transfers between devices: 3.84 us -> 0.01 us  [row_values(): lax.ppermute(piece, 'val', [(i, i ^ bits) for i in range(groups)])]
    ppermute x3 -> x5, starting transfers between devices: 5.25 us -> 8.17 us  [the longest x3 5.28 us: row_values(): other = lax.ppermute(piece, 'grid', ring)]
  transfers between devices with their start and end apart: 14 -> 14, of which waited for: 5 -> 7; matrix products, arithmetic and copies ran while one was open for 5% -> 4% of each run, Pallas kernels for 0% -> 0%
where the time goes in v4:
time: 93.5 us; the launch traced here: 93.1 us
  starting transfers between devices  33 us (35%)
  Pallas kernels  26.2 us (28%)
  waiting for transfers between devices  20.8 us (22%)
  local copies, waits for them, and re-layouts  6.19 us (7%)
  other arithmetic  3.85 us (4%)
  matrix products  2.79 us (3%)
    pallas_call x1, Pallas kernels, picked_partials(): pl.pallas_call(spectra_kernel, out_shape=[jax.ShapeDtypeStruct((slabs, va...  26.2 us
    ppermute x5, waiting for transfers between devices, swap(): other = lax.ppermute(value, axis, [(i, partner(i)) for i in range(count)])  16.4 us
    ppermute x5, starting transfers between devices, swap(): other = lax.ppermute(value, axis, [(i, partner(i)) for i in range(count)])  12.2 us
    all_to_all x1, starting transfers between devices, column_values(): lax.all_to_all(partials.reshape(groups * slabs, piece, width), ('cond', '...  7.5 us
    ppermute x3, starting transfers between devices, row_values(): other = lax.ppermute(piece, 'grid', ring)  5.28 us
    ppermute x3, starting transfers between devices, row_values(): lax.ppermute(piece, 'val', [(i, i ^ bits) for i in range(groups)])  5.13 us
    ppermute x3, waiting for transfers between devices, row_values(): other = lax.ppermute(piece, 'grid', ring)  3.71 us
    dot_general x1, matrix products, local(): lax.dot_general(left, columns, (((0,), (0,)), ((), ())), preferred_elemen...  2.79 us
  transfers between devices with their start and end apart: 14, of which 7 were waited for; matrix products, arithmetic and copies ran while one was open for 4% of the time, Pallas kernels for 0%

profile of v4, /device:TPU:1, one launch (start us, length us, event | category | flops | bytes accessed | tf_op | source)
XLA Modules:
  0.0 93.1 jit_solution(10564718302999357132)
XLA Ops:
  0.0 0.8 fusion.7
  0.8 1.5 %constant_dynamic-slice_fusion.1.phase_ref = bf16[2,96,24]{2,1,0:T(8,128)(2,1)} fusion(bf16[2,96,96]{2,1,0:T(8,128)(2,1)} %constant.179.clone, s32[]{:T(128)S(6)} %select_n.289), kind=kLoop, calls=%fused_computation.67 | loop fusion | bytes 18436 | tf_op jit(solution)/shard_map/dynamic_slice | solution.py:251
  3.0 26.2 %spectra.1 = (bf16[4,4,32,384]{3,2,1,0:T(8,128)(2,1)}, bf16[8,4,8,768]{3,2,1,0:T(8,128)(2,1)}) custom-call(s32[48,2,128]{2,1,0:T(2,128)} %pad_add_fusion.index_ref, bf16[4,24,9216]{2,1,0:T(8,128)(2,1)} %val_ref.1, bf16[4,24,9216]{2,1,0:T(8,128)(2,1)} %cond_ref.1, bf16[2,96,24]{2,1,0:T(8,128)(2,1)} %constant_dynamic-slice_fusion.1.phase_ref, ...), custom_call_target="tpu_custom_call" | custom-call | tf_op jit(solution)/shard_map/spectra/pallas_call | solution.py:273
  29.3 1.0 %dynamic-slice_bitcast_fusion.2 = (bf16[4,32,384]{2,1,0:T(8,128)(2,1)S(1)}, bf16[4,32,384]{2,1,0:T(8,128)(2,1)S(1)}, bf16[4,32,384]{2,1,0:T(8,128)(2,1)S(1)}) fusion(bf16[4,4,32,384]{3,2,1,0:T(8,128)(2,1)} %get-tuple-element.7, s32[]{:T(128)S(6)} %select_n.292, s32[]{:T(128)S(6)} %select_n.296, s32[]{:T(128)S(6)} %select_n.294), kind=kLoop, calls=%fused_computation.28 | loop fusion | bytes 589836 | tf_op jit(solution)/shard_map/jit(dynamic_index_in_dim)/squeeze | solution.py:314
  30.3 2.2 %collective-permute-start = (bf16[4,32,384]{2,1,0:T(8,128)(2,1)S(1)}, bf16[4,32,384]{2,1,0:T(8,128)(2,1)S(1)}, u32[]{:S(2)}, u32[]{:S(2)}) collective-permute-start(bf16[4,32,384]{2,1,0:T(8,128)(2,1)S(1)} %get-tuple-element.15), channel_id=1, source_target_pairs={{0,1},{1,2},{2,3},{3,0},{4,5},{5,6},{6,7},{7,4},{8,9},{9,10},{10,1... | collective-permute-start | bytes 294920 | tf_op jit(solution)/shard_map/ppermute | solution.py:316
  32.5 1.5 %collective-permute-start.2 = (bf16[4,32,384]{2,1,0:T(8,128)(2,1)S(1)}, bf16[4,32,384]{2,1,0:T(8,128)(2,1)S(1)}, u32[]{:S(2)}, u32[]{:S(2)}) collective-permute-start(bf16[4,32,384]{2,1,0:T(8,128)(2,1)S(1)} %get-tuple-element.16), channel_id=1, source_target_pairs={{0,3},{1,0},{2,1},{3,2},{4,7},{5,4},{6,5},{7,6},{8,11},{9,8},{10,9... | collective-permute-start | bytes 294920 | tf_op jit(solution)/shard_map/ppermute | solution.py:316
  34.0 1.6 %collective-permute-start.1 = (bf16[4,32,384]{2,1,0:T(8,128)(2,1)S(1)}, bf16[4,32,384]{2,1,0:T(8,128)(2,1)S(1)}, u32[]{:S(2)}, u32[]{:S(2)}) collective-permute-start(bf16[4,32,384]{2,1,0:T(8,128)(2,1)S(1)} %get-tuple-element.17), channel_id=1, source_target_pairs={{0,2},{1,3},{2,0},{3,1},{4,6},{5,7},{6,4},{7,5},{8,10},{9,11},{10,... | collective-permute-start | bytes 294920 | tf_op jit(solution)/shard_map/ppermute | solution.py:316
  36.3 3.0 %collective-permute-done.1 = bf16[4,32,384]{2,1,0:T(8,128)(2,1)S(1)} collective-permute-done((bf16[4,32,384]{2,1,0:T(8,128)(2,1)S(1)}, bf16[4,32,384]{2,1,0:T(8,128)(2,1)S(1)}, u32[]{:S(2)}, u32[]{:S(2)}) %collective-permute-start.1) | collective-permute-done | bytes 98336 | tf_op jit(solution)/shard_map/ppermute | solution.py:316
  39.3 0.9 %fusion.4 = bf16[4,32,384]{2,1,0:T(8,128)(2,1)S(1)} fusion(bf16[4,32,384]{2,1,0:T(8,128)(2,1)S(1)} %collective-permute-done.2, bf16[4,32,384]{2,1,0:T(8,128)(2,1)S(1)} %collective-permute-done.1, bf16[4,32,384]{2,1,0:T(8,128)(2,1)S(1)} %collective-permute-done, bf16[4,4,32,384]{3,2,1,0:T(8,128)(2,1)} %get-tuple-element.7, s32[]{:T(128)S(6)} %select_n.290), kind=kLoop, calls=%fused_computation.18 | loop fusion | flops 393216 | bytes 491524 | tf_op jit(solution)/shard_map/convert_element_type | solution.py:318
  40.3 4.6 %collective-permute-start.5 = (bf16[32,384]{1,0:T(8,128)(2,1)S(1)}, bf16[32,384]{1,0:T(8,128)(2,1)S(1)}, u32[]{:S(2)}, u32[]{:S(2)}) collective-permute-start(bf16[32,384]{1,0:T(8,128)(2,1)S(1)} %get-tuple-element.19), channel_id=1, source_target_pairs={{0,96},{32,64},{64,32},{96,0},{1,97},{33,65},{65,33},{97,1},{2,98}... | collective-permute-start | bytes 73736 | tf_op jit(solution)/shard_map/ppermute | solution.py:322
  45.4 7.5 %all-to-all-start = ((bf16[32,8,768]{2,1,0:T(8,128)(2,1)}), bf16[32,8,768]{2,1,0:T(8,128)(2,1)S(1)}, u32[]{:S(2)}, u32[]{:S(2)}) async-start(bf16[32,8,768]{2,1,0:T(8,128)(2,1)} %bitcast.52), calls=%async_computation | async-start | bytes 786432 | tf_op jit(solution)/shard_map/all_to_all | solution.py:358
  53.1 1.3 %collective-permute-start.6 = (bf16[1,4,32,384]{3,2,1,0:T(8,128)(2,1)S(1)}, bf16[1,4,32,384]{3,2,1,0:T(8,128)(2,1)S(1)}, u32[]{:S(2)}, u32[]{:S(2)}) collective-permute-start(bf16[1,4,32,384]{3,2,1,0:T(8,128)(2,1)S(1)} %bitcast.49), channel_id=1, source_target_pairs={{0,4},{4,0},{8,12},{12,8},{16,20},{20,16},{24,28},{28,24},{1,5},{5... | collective-permute-start | bytes 294920 | tf_op jit(solution)/shard_map/ppermute | solution.py:303
  54.9 5.7 %collective-permute-done.6 = bf16[1,4,32,384]{3,2,1,0:T(8,128)(2,1)S(1)} collective-permute-done((bf16[1,4,32,384]{3,2,1,0:T(8,128)(2,1)S(1)}, bf16[1,4,32,384]{3,2,1,0:T(8,128)(2,1)S(1)}, u32[]{:S(2)}, u32[]{:S(2)}) %collective-permute-start.6) | collective-permute-done | bytes 98336 | tf_op jit(solution)/shard_map/ppermute | solution.py:303
  60.6 2.5 %collective-permute-start.7 = (bf16[2,4,32,384]{3,2,1,0:T(8,128)(2,1)S(1)}, bf16[2,4,32,384]{3,2,1,0:T(8,128)(2,1)S(1)}, u32[]{:S(2)}, u32[]{:S(2)}) collective-permute-start(bf16[2,4,32,384]{3,2,1,0:T(8,128)(2,1)S(1)} %maximum_select_fusion.5), channel_id=1, source_target_pairs={{0,8},{4,12},{8,0},{12,4},{16,24},{20,28},{24,16},{28,20},{32,56},... | collective-permute-start | bytes 589832 | tf_op jit(solution)/shard_map/ppermute | solution.py:339
  63.2 2.5 %collective-permute-start.9 = (bf16[1,64,768]{2,1,0:T(8,128)(2,1)S(1)}, bf16[1,64,768]{2,1,0:T(8,128)(2,1)S(1)}, u32[]{:S(2)}, u32[]{:S(2)}) collective-permute-start(bf16[1,64,768]{2,1,0:T(8,128)(2,1)S(1)} %bitcast.55), channel_id=1, source_target_pairs={{0,64},{32,96},{64,0},{96,32},{1,65},{33,97},{65,1},{97,33},{2,66}... | collective-permute-start | bytes 294920 | tf_op jit(solution)/shard_map/ppermute | solution.py:303
  66.8 1.5 %collective-permute-done.9 = bf16[1,64,768]{2,1,0:T(8,128)(2,1)S(1)} collective-permute-done((bf16[1,64,768]{2,1,0:T(8,128)(2,1)S(1)}, bf16[1,64,768]{2,1,0:T(8,128)(2,1)S(1)}, u32[]{:S(2)}, u32[]{:S(2)}) %collective-permute-start.9) | collective-permute-done | bytes 98336 | tf_op jit(solution)/shard_map/ppermute | solution.py:303
  68.3 1.3 %collective-permute-start.10 = (bf16[2,64,768]{2,1,0:T(8,128)(2,1)S(1)}, bf16[2,64,768]{2,1,0:T(8,128)(2,1)S(1)}, u32[]{:S(2)}, u32[]{:S(2)}) collective-permute-start(bf16[2,64,768]{2,1,0:T(8,128)(2,1)S(1)} %maximum_select_fusion.6), channel_id=1, source_target_pairs={{0,1},{1,0},{2,3},{3,2},{4,5},{5,4},{6,7},{7,6},{8,9},{9,8},{10,11... | collective-permute-start | bytes 589832 | tf_op jit(solution)/shard_map/ppermute | solution.py:303
  69.6 3.6 %collective-permute-done.10 = bf16[2,64,768]{2,1,0:T(8,128)(2,1)S(1)} collective-permute-done((bf16[2,64,768]{2,1,0:T(8,128)(2,1)S(1)}, bf16[2,64,768]{2,1,0:T(8,128)(2,1)S(1)}, u32[]{:S(2)}, u32[]{:S(2)}) %collective-permute-start.10) | collective-permute-done | bytes 196640 | tf_op jit(solution)/shard_map/ppermute | solution.py:303
  73.3 2.5 %collective-permute-start.11 = (bf16[4,64,768]{2,1,0:T(8,128)(2,1)S(1)}, bf16[4,64,768]{2,1,0:T(8,128)(2,1)S(1)}, u32[]{:S(2)}, u32[]{:S(2)}) collective-permute-start(bf16[4,64,768]{2,1,0:T(8,128)(2,1)S(1)} %maximum_select_fusion.3), channel_id=1, source_target_pairs={{0,3},{1,2},{2,1},{3,0},{4,7},{5,6},{6,5},{7,4},{8,11},{9,10},{10,... | collective-permute-start | bytes 1179656 | tf_op jit(solution)/shard_map/ppermute | solution.py:303
  76.2 5.6 %collective-permute-done.11 = bf16[4,64,768]{2,1,0:T(8,128)(2,1)S(1)} collective-permute-done((bf16[4,64,768]{2,1,0:T(8,128)(2,1)S(1)}, bf16[4,64,768]{2,1,0:T(8,128)(2,1)S(1)}, u32[]{:S(2)}, u32[]{:S(2)}) %collective-permute-start.11) | collective-permute-done | bytes 393248 | tf_op jit(solution)/shard_map/ppermute | solution.py:303
  81.9 4.6 %collective-permute-start.12 = (bf16[8,64,768]{2,1,0:T(8,128)(2,1)S(1)}, bf16[8,64,768]{2,1,0:T(8,128)(2,1)S(1)}, u32[]{:S(2)}, u32[]{:S(2)}) collective-permute-start(bf16[8,64,768]{2,1,0:T(8,128)(2,1)S(1)} %maximum_select_fusion.1), channel_id=1, source_target_pairs={{0,32},{32,0},{64,96},{96,64},{1,33},{33,1},{65,97},{97,65},{2,34}... | collective-permute-start | bytes 2359304 | tf_op jit(solution)/shard_map/ppermute | solution.py:303
  87.2 1.6 %copy.29 = bf16[768,1024]{1,0:T(8,128)(2,1)} copy(bf16[768,1024]{0,1:T(8,128)(2,1)S(1)} %maximum_bitcast_fusion) | data formatting | bytes 3145728 | tf_op jit(solution)/shard_map/dot_general | solution.py:398
  89.1 1.2 %copy-done = bf16[768,1024]{1,0:T(8,128)(2,1)S(1)} copy-done((bf16[768,1024]{1,0:T(8,128)(2,1)S(1)}, bf16[768,1024]{1,0:T(8,128)(2,1)}, u32[]{:S(2)}) %copy-start) | copy-done | bytes 1572888
  90.3 2.8 %fusion.24 = f32[2,384,768]{2,1,0:T(8,128)} fusion(bf16[2,384,1024]{2,1,0:T(8,128)(2,1)S(1)} %bitcast.47, bf16[1024,768,1]{1,0,2:T(8,128)(2,1)S(1)} %bitcast.48), kind=kOutput, calls=%fused_computation.69 | convolution fusion | flops 1207959552 | bytes 5505024 | tf_op jit(solution)/shard_map/dot_general | solution.py:398
  (49 shorter events, 5.2 us)
Async XLA Ops:
  29.3 25.1 %copy-start.1 = (f32[16]{0:T(128)S(1)}, f32[16]{0:T(128)}, u32[]{:S(2)}) copy-start(f32[16]{0:T(128)} %param.13) | copy-start | bytes 196
  29.3 25.2 %copy-start.2 = (f32[32]{0:T(128)S(1)}, f32[32]{0:T(128)}, u32[]{:S(2)}) copy-start(f32[32]{0:T(128)} %param.14) | copy-start | bytes 388
  30.3 6.0 %collective-permute-start = (bf16[4,32,384]{2,1,0:T(8,128)(2,1)S(1)}, bf16[4,32,384]{2,1,0:T(8,128)(2,1)S(1)}, u32[]{:S(2)}, u32[]{:S(2)}) collective-permute-start(bf16[4,32,384]{2,1,0:T(8,128)(2,1)S(1)} %get-tuple-element.15), channel_id=1, source_target_pairs={{0,1},{1,2},{2,3},{3,0},{4,5},{5,6},{6,7},{7,4},{8,9},{9,10},{10,1... | collective-permute-start | bytes 294920 | tf_op jit(solution)/shard_map/ppermute | solution.py:316
  32.5 3.9 %collective-permute-start.2 = (bf16[4,32,384]{2,1,0:T(8,128)(2,1)S(1)}, bf16[4,32,384]{2,1,0:T(8,128)(2,1)S(1)}, u32[]{:S(2)}, u32[]{:S(2)}) collective-permute-start(bf16[4,32,384]{2,1,0:T(8,128)(2,1)S(1)} %get-tuple-element.16), channel_id=1, source_target_pairs={{0,3},{1,0},{2,1},{3,2},{4,7},{5,4},{6,5},{7,6},{8,11},{9,8},{10,9... | collective-permute-start | bytes 294920 | tf_op jit(solution)/shard_map/ppermute | solution.py:316
  34.0 5.3 %collective-permute-start.1 = (bf16[4,32,384]{2,1,0:T(8,128)(2,1)S(1)}, bf16[4,32,384]{2,1,0:T(8,128)(2,1)S(1)}, u32[]{:S(2)}, u32[]{:S(2)}) collective-permute-start(bf16[4,32,384]{2,1,0:T(8,128)(2,1)S(1)} %get-tuple-element.17), channel_id=1, source_target_pairs={{0,2},{1,3},{2,0},{3,1},{4,6},{5,7},{6,4},{7,5},{8,10},{9,11},{10,... | collective-permute-start | bytes 294920 | tf_op jit(solution)/shard_map/ppermute | solution.py:316
  40.3 12.7 %collective-permute-start.5 = (bf16[32,384]{1,0:T(8,128)(2,1)S(1)}, bf16[32,384]{1,0:T(8,128)(2,1)S(1)}, u32[]{:S(2)}, u32[]{:S(2)}) collective-permute-start(bf16[32,384]{1,0:T(8,128)(2,1)S(1)} %get-tuple-element.19), channel_id=1, source_target_pairs={{0,96},{32,64},{64,32},{96,0},{1,97},{33,65},{65,33},{97,1},{2,98}... | collective-permute-start | bytes 73736 | tf_op jit(solution)/shard_map/ppermute | solution.py:322
  44.9 8.0 %collective-permute-start.4 = (bf16[32,384]{1,0:T(8,128)(2,1)S(1)}, bf16[32,384]{1,0:T(8,128)(2,1)S(1)}, u32[]{:S(2)}, u32[]{:S(2)}) collective-permute-start(bf16[32,384]{1,0:T(8,128)(2,1)S(1)} %get-tuple-element.20), channel_id=1, source_target_pairs={{0,64},{32,96},{64,0},{96,32},{1,65},{33,97},{65,1},{97,33},{2,66}... | collective-permute-start | bytes 73736 | tf_op jit(solution)/shard_map/ppermute | solution.py:322
  45.0 7.9 %collective-permute-start.3 = (bf16[32,384]{1,0:T(8,128)(2,1)S(1)}, bf16[32,384]{1,0:T(8,128)(2,1)S(1)}, u32[]{:S(2)}, u32[]{:S(2)}) collective-permute-start(bf16[32,384]{1,0:T(8,128)(2,1)S(1)} %get-tuple-element.21), channel_id=1, source_target_pairs={{0,32},{32,0},{64,96},{96,64},{1,33},{33,1},{65,97},{97,65},{2,34}... | collective-permute-start | bytes 73736 | tf_op jit(solution)/shard_map/ppermute | solution.py:322
  45.4 17.8 %all-to-all-start = ((bf16[32,8,768]{2,1,0:T(8,128)(2,1)}), bf16[32,8,768]{2,1,0:T(8,128)(2,1)S(1)}, u32[]{:S(2)}, u32[]{:S(2)}) async-start(bf16[32,8,768]{2,1,0:T(8,128)(2,1)} %bitcast.52), calls=%async_computation | async-start | bytes 786432 | tf_op jit(solution)/shard_map/all_to_all | solution.py:358
  53.1 7.5 %collective-permute-start.6 = (bf16[1,4,32,384]{3,2,1,0:T(8,128)(2,1)S(1)}, bf16[1,4,32,384]{3,2,1,0:T(8,128)(2,1)S(1)}, u32[]{:S(2)}, u32[]{:S(2)}) collective-permute-start(bf16[1,4,32,384]{3,2,1,0:T(8,128)(2,1)S(1)} %bitcast.49), channel_id=1, source_target_pairs={{0,4},{4,0},{8,12},{12,8},{16,20},{20,16},{24,28},{28,24},{1,5},{5... | collective-permute-start | bytes 294920 | tf_op jit(solution)/shard_map/ppermute | solution.py:303
  60.6 5.8 %collective-permute-start.7 = (bf16[2,4,32,384]{3,2,1,0:T(8,128)(2,1)S(1)}, bf16[2,4,32,384]{3,2,1,0:T(8,128)(2,1)S(1)}, u32[]{:S(2)}, u32[]{:S(2)}) collective-permute-start(bf16[2,4,32,384]{3,2,1,0:T(8,128)(2,1)S(1)} %maximum_select_fusion.5), channel_id=1, source_target_pairs={{0,8},{4,12},{8,0},{12,4},{16,24},{20,28},{24,16},{28,20},{32,56},... | collective-permute-start | bytes 589832 | tf_op jit(solution)/shard_map/ppermute | solution.py:339
  63.2 5.1 %collective-permute-start.9 = (bf16[1,64,768]{2,1,0:T(8,128)(2,1)S(1)}, bf16[1,64,768]{2,1,0:T(8,128)(2,1)S(1)}, u32[]{:S(2)}, u32[]{:S(2)}) collective-permute-start(bf16[1,64,768]{2,1,0:T(8,128)(2,1)S(1)} %bitcast.55), channel_id=1, source_target_pairs={{0,64},{32,96},{64,0},{96,32},{1,65},{33,97},{65,1},{97,33},{2,66}... | collective-permute-start | bytes 294920 | tf_op jit(solution)/shard_map/ppermute | solution.py:303
  66.5 9.4 %collective-permute-start.8 = (bf16[2,2,4,32,384]{4,3,2,1,0:T(8,128)(2,1)S(1)}, bf16[2,2,4,32,384]{4,3,2,1,0:T(8,128)(2,1)S(1)}, u32[]{:S(2)}, u32[]{:S(2)}) collective-permute-start(bf16[2,2,4,32,384]{4,3,2,1,0:T(8,128)(2,1)S(1)} %maximum_select_fusion.2), channel_id=1, source_target_pairs={{0,24},{4,28},{8,16},{12,20},{16,8},{20,12},{24,0},{28,4},{32,40},... | collective-permute-start | bytes 1179656 | tf_op jit(solution)/shard_map/ppermute | solution.py:342
  68.3 4.9 %collective-permute-start.10 = (bf16[2,64,768]{2,1,0:T(8,128)(2,1)S(1)}, bf16[2,64,768]{2,1,0:T(8,128)(2,1)S(1)}, u32[]{:S(2)}, u32[]{:S(2)}) collective-permute-start(bf16[2,64,768]{2,1,0:T(8,128)(2,1)S(1)} %maximum_select_fusion.6), channel_id=1, source_target_pairs={{0,1},{1,0},{2,3},{3,2},{4,5},{5,4},{6,7},{7,6},{8,9},{9,8},{10,11... | collective-permute-start | bytes 589832 | tf_op jit(solution)/shard_map/ppermute | solution.py:303
  73.3 8.5 %collective-permute-start.11 = (bf16[4,64,768]{2,1,0:T(8,128)(2,1)S(1)}, bf16[4,64,768]{2,1,0:T(8,128)(2,1)S(1)}, u32[]{:S(2)}, u32[]{:S(2)}) collective-permute-start(bf16[4,64,768]{2,1,0:T(8,128)(2,1)S(1)} %maximum_select_fusion.3), channel_id=1, source_target_pairs={{0,3},{1,2},{2,1},{3,0},{4,7},{5,6},{6,5},{7,4},{8,11},{9,10},{10,... | collective-permute-start | bytes 1179656 | tf_op jit(solution)/shard_map/ppermute | solution.py:303
  81.9 7.0 %collective-permute-start.12 = (bf16[8,64,768]{2,1,0:T(8,128)(2,1)S(1)}, bf16[8,64,768]{2,1,0:T(8,128)(2,1)S(1)}, u32[]{:S(2)}, u32[]{:S(2)}) collective-permute-start(bf16[8,64,768]{2,1,0:T(8,128)(2,1)S(1)} %maximum_select_fusion.1), channel_id=1, source_target_pairs={{0,32},{32,0},{64,96},{96,64},{1,33},{33,1},{65,97},{97,65},{2,34}... | collective-permute-start | bytes 2359304 | tf_op jit(solution)/shard_map/ppermute | solution.py:303
  88.9 1.4 %copy-start = (bf16[768,1024]{1,0:T(8,128)(2,1)S(1)}, bf16[768,1024]{1,0:T(8,128)(2,1)}, u32[]{:S(2)}) copy-start(bf16[768,1024]{1,0:T(8,128)(2,1)} %copy.29) | copy-start | bytes 4718596
